TPU v7x, 1024 devices: a whole 4x8x16 slice. The times are simulated.
1024 devices in a mesh: gz: 64 (over y_lo, z), gx: 4 (over y_hi, core), gy: 4 (over x).
Axes of the slice: x: 4, y: 8 (y_hi: 2, y_lo: 4; y = y_hi * 4 + y_lo), z: 16, core: 2. Of those that a mesh axis runs over, the one named last changes fastest.
Arguments:
- fields_in: float32 [6, 256, 256, 512], P(None, 'gz', 'gx', 'gy'), may hold values from -6 to 6
- material: int32 [256, 256, 512], P('gz', 'gx', 'gy'), may hold values from 0 to 3, as said below
- material_eps: float32 [4], replicated, may hold values from 1 to 12
- source_plane: int32 [1], replicated, may hold values from 0 to 255
- source_wave: float32 [4], replicated, may hold values from -8 to 8
- source_profile: float32 [256, 512], P('gx', 'gy'), may hold values from -6 to 6
- forward_fields: bfloat16 [4, 3, 256, 256, 512], P(None, None, 'gz', 'gx', 'gy'), may hold values from -6 to 6
Outputs:
- fields_out: float32 [6, 256, 256, 512], P(None, 'gz', 'gx', 'gy')
- eps_grad: float32 [256, 256, 512], P('gz', 'gx', 'gy')
Inputs may be any that keep to these rules, and one draw needn't show every extreme that they name: `material`: planes z below 96 hold index 1; planes from 160 up hold index 0; the planes between hold 0 or an index of 2 to 3 in each cell.
All inputs are finite; a program needn't handle non-finite values.
Results may differ from a plain program's by a relative error of at most 0.0003.
Values sent between devices are 32-bit elements; how exact they have to be, the bound alone decides.
A program may use at most 64 MiB of HBM per device.

v0:
```python
import jax
import jax.numpy as jnp
from jax import lax
from jax.sharding import PartitionSpec as P

COURANT = 0.5


def from_behind(block, axis, distance):
    devices = range(lax.axis_size(axis))
    route = [(i - distance, i) for i in devices if i - distance in devices]
    return lax.ppermute(block, axis, route)


def passed_along(array, axis, by):
    length = lax.axis_size(axis)
    return lax.ppermute(array, axis, [(i, (i + by) % length) for i in range(length)])


def z_neighbour(planes, offset):
    if offset < 0:
        border = planes[:, :1]
    else:
        border = planes[:, -1:]
    arrived = from_behind(border, "gz", offset)
    if offset < 0:
        return jnp.concatenate([planes[:, 1:], arrived], axis=1)
    return jnp.concatenate([arrived, planes[:, :-1]], axis=1)


def x_neighbour(planes, offset):
    if offset < 0:
        border = planes[:, :, :1]
    else:
        border = planes[:, :, -1:]
    arrived = passed_along(border, "gx", offset)
    if offset < 0:
        return jnp.concatenate([planes[:, :, 1:], arrived], axis=2)
    return jnp.concatenate([arrived, planes[:, :, :-1]], axis=2)


def y_neighbour(planes, offset):
    if offset < 0:
        border = planes[:, :, :, :1]
    else:
        border = planes[:, :, :, -1:]
    arrived = passed_along(border, "gy", offset)
    if offset < 0:
        return jnp.concatenate([planes[:, :, :, 1:], arrived], axis=3)
    return jnp.concatenate([arrived, planes[:, :, :, :-1]], axis=3)


def yee_step(electric, magnetic, coef, source, amplitude, z_side, x_side, y_side):
    elec_x, elec_y, elec_z = (electric[0], electric[1], electric[2])
    z_next = z_side(jnp.stack([elec_x, elec_y]), -1)
    x_next = x_side(jnp.stack([elec_y, elec_z]), -1)
    y_next = y_side(jnp.stack([elec_x, elec_z]), -1)
    curl_x = y_next[1] - elec_z - (z_next[1] - elec_y)
    curl_y = z_next[0] - elec_x - (x_next[1] - elec_z)
    curl_z = x_next[0] - elec_y - (y_next[0] - elec_x)
    magn_x = magnetic[0] - COURANT * curl_x
    magn_y = magnetic[1] - COURANT * curl_y
    magn_z = magnetic[2] - COURANT * curl_z
    z_prev = z_side(jnp.stack([magn_x, magn_y]), 1)
    x_prev = x_side(jnp.stack([magn_y, magn_z]), 1)
    y_prev = y_side(jnp.stack([magn_x, magn_z]), 1)
    back_x = magn_z - y_prev[1] - (magn_y - z_prev[1])
    back_y = magn_x - z_prev[0] - (magn_z - x_prev[1])
    back_z = magn_y - x_prev[0] - (magn_x - y_prev[0])
    new_x = elec_x + coef * back_x + coef * amplitude * source
    new_y = elec_y + coef * back_y
    new_z = elec_z + coef * back_z
    return (jnp.stack([new_x, new_y, new_z]), jnp.stack([magn_x, magn_y, magn_z]))


def accumulate(grad, stored, electric):
    stored = stored.astype(jnp.float32)
    return grad + stored[0] * electric[0] + stored[1] * electric[1] + stored[2] * electric[2]


def on_device(
    fields_in, material, material_eps, source_plane, source_wave, source_profile, forward_fields
):
    depth, width_x, width_y = material.shape
    permit = jnp.zeros(material.shape, jnp.float32)
    for which in range(material_eps.shape[0]):
        permit = permit + jnp.where(material == which, material_eps[which], 0.0)
    coef = COURANT / permit
    zpos = lax.axis_index("gz") * depth + jnp.arange(depth)
    source = (
        jnp.where(zpos == source_plane[0], 1.0, 0.0).astype(jnp.float32)[:, None, None]
        * source_profile[None]
    )
    count = source_wave.shape[0]
    grad = jnp.zeros(material.shape, jnp.float32)
    stacked = jnp.concatenate([fields_in, coef[None], source[None]], axis=0)
    electric = stacked[0:3]
    magnetic = stacked[3:6]
    wide_coef = stacked[6]
    wide_source = stacked[7]
    for instant in range(count):
        electric, magnetic = yee_step(
            electric,
            magnetic,
            wide_coef,
            wide_source,
            source_wave[instant],
            z_neighbour,
            x_neighbour,
            y_neighbour,
        )
        grad = accumulate(grad, forward_fields[instant], electric)
    fields_out = jnp.concatenate([electric, magnetic], axis=0)
    eps_grad = jnp.where(material >= 2, -grad, 0.0)
    return (fields_out, eps_grad)


def solution(mesh):
    placed = (
        P(None, "gz", "gx", "gy"),
        P("gz", "gx", "gy"),
        P(),
        P(),
        P(),
        P("gx", "gy"),
        P(None, None, "gz", "gx", "gy"),
    )
    return jax.shard_map(
        on_device,
        mesh=mesh,
        in_specs=placed,
        out_specs=(P(None, "gz", "gx", "gy"), P("gz", "gx", "gy")),
        check_vma=False,
    )
```

profile of v0, /device:TPU:9, one launch (start us, length us, event | category | flops | bytes accessed | tf_op | source)
XLA Modules:
  0.0 191.3 jit_solution(3424852815091762897)
XLA Ops:
  0.6 0.8 slice.411
  1.5 2.6 %collective-permute-start = (f32[2,4,1,128]{3,2,1,0:T(1,128)S(1)}, f32[2,4,1,128]{3,2,1,0:T(1,128)S(1)}, u32[]{:S(2)}, u32[]{:S(2)}) collective-permute-start(f32[2,4,1,128]{3,2,1,0:T(1,128)S(1)} %slice.411), channel_id=1, source_target_pairs={{0,12},{4,0},{8,4},{12,8},{1,13},{5,1},{9,5},{13,9},{2,14},{6,2},{... | collective-permute-start | bytes 12296 | tf_op jit(solution)/shard_map/ppermute | solution.py:17
  4.1 0.8 slice.421
  4.9 17.8 %collective-permute-start.2 = (f32[2,1,64,128]{3,2,1,0:T(8,128)S(1)}, f32[2,1,64,128]{3,2,1,0:T(8,128)S(1)}, u32[]{:S(2)}, u32[]{:S(2)}) collective-permute-start(f32[2,1,64,128]{3,2,1,0:T(8,128)S(1)} %slice.421), channel_id=1, source_target_pairs={{16,0},{32,16},{48,32},{64,48},{80,64},{96,80},{112,96},{128,112},... | collective-permute-start | bytes 196616 | tf_op jit(solution)/shard_map/ppermute | solution.py:12
  22.7 1.5 fusion.213
  24.2 1.5 fusion.212
  25.6 0.9 slice.420
  26.6 1.0 slice.410
  28.3 4.4 %collective-permute-start.1 = (f32[2,4,64,1]{3,2,1,0:T(8,128)S(1)}, f32[2,4,64,1]{3,2,1,0:T(8,128)S(1)}, u32[]{:S(2)}, u32[]{:S(2)}) collective-permute-start(f32[2,4,64,1]{3,2,1,0:T(8,128)S(1)} %pad_maximum_fusion.15), channel_id=1, source_target_pairs={{0,3},{1,0},{2,1},{3,2},{4,7},{5,4},{6,5},{7,6},{8,11},{9,8},{10,9... | collective-permute-start | bytes 6152 | tf_op jit(solution)/shard_map/ppermute | solution.py:17
  32.7 0.1 slice_maximum_fusion
  32.9 3.2 %collective-permute-done.1 = f32[2,4,64,1]{3,2,1,0:T(8,128)S(1)} collective-permute-done((f32[2,4,64,1]{3,2,1,0:T(8,128)S(1)}, f32[2,4,64,1]{3,2,1,0:T(8,128)S(1)}, u32[]{:S(2)}, u32[]{:S(2)}) %collective-permute-start.1) | collective-permute-done | bytes 2080 | tf_op jit(solution)/shard_map/ppermute | solution.py:17
  36.0 0.2 multiply_subtract_fusion.2
  36.2 0.1 fusion.3
  36.3 10.5 %collective-permute-start.5 = (f32[2,4,1,128]{3,2,1,0:T(1,128)S(1)}, f32[2,4,1,128]{3,2,1,0:T(1,128)S(1)}, u32[]{:S(2)}, u32[]{:S(2)}) collective-permute-start(f32[2,4,1,128]{3,2,1,0:T(1,128)S(1)} %fusion.205), channel_id=1, source_target_pairs={{0,4},{4,8},{8,12},{12,0},{1,5},{5,9},{9,13},{13,1},{2,6},{6,10},{... | collective-permute-start | bytes 12296 | tf_op jit(solution)/shard_map/ppermute | solution.py:17
  46.9 1.9 %collective-permute-start.4 = (f32[2,1,64,128]{3,2,1,0:T(8,128)S(1)}, f32[2,1,64,128]{3,2,1,0:T(8,128)S(1)}, u32[]{:S(2)}, u32[]{:S(2)}) collective-permute-start(f32[2,1,64,128]{3,2,1,0:T(8,128)S(1)} %fusion.201), channel_id=1, source_target_pairs={{0,16},{16,32},{32,48},{48,64},{64,80},{80,96},{96,112},{112,128},... | collective-permute-start | bytes 196616 | tf_op jit(solution)/shard_map/ppermute | solution.py:12
  48.8 2.8 %collective-permute-start.3 = (f32[2,4,64,1]{3,2,1,0:T(8,128)S(1)}, f32[2,4,64,1]{3,2,1,0:T(8,128)S(1)}, u32[]{:S(2)}, u32[]{:S(2)}) collective-permute-start(f32[2,4,64,1]{3,2,1,0:T(8,128)S(1)} %fusion.3), channel_id=1, source_target_pairs={{0,1},{1,2},{2,3},{3,0},{4,5},{5,6},{6,7},{7,4},{8,9},{9,10},{10,1... | collective-permute-start | bytes 6152 | tf_op jit(solution)/shard_map/ppermute | solution.py:17
  51.7 7.0 %collective-permute-done.3 = f32[2,4,64,1]{3,2,1,0:T(8,128)S(1)} collective-permute-done((f32[2,4,64,1]{3,2,1,0:T(8,128)S(1)}, f32[2,4,64,1]{3,2,1,0:T(8,128)S(1)}, u32[]{:S(2)}, u32[]{:S(2)}) %collective-permute-start.3) | collective-permute-done | bytes 2080 | tf_op jit(solution)/shard_map/ppermute | solution.py:17
  58.7 0.1 fusion.21
  58.8 2.7 %fusion.182 = (f32[4,64,128]{2,1,0:T(8,128)S(1)}, f32[4,64,128]{2,1,0:T(8,128)S(1)}, f32[4,64,128]{2,1,0:T(8,128)S(1)}) fusion(f32[2,4,64,128]{3,2,1,0:T(8,128)S(1)} %get-tuple-element.45, f32[2,4,64,128]{3,2,1,0:T(8,128)S(1)} %get-tuple-element.44, f32[6,4,64,128]{3,2,1,0:T(8,128)S(1)} %copy-done, f32[]{:T(128)} %bitcast.4, ...), kind=kLoop, calls=%fused_computation.312 | loop fusion | flops 983040 | bytes 2359312 | tf_op jit(solution)/shard_map/add | solution.py:71
  61.5 2.6 %fusion.177 = (f32[4,64,128]{2,1,0:T(8,128)S(1)}, f32[4,64,128]{2,1,0:T(8,128)S(1)}) fusion(f32[4,64,128]{2,1,0:T(8,128)S(1)} %get-tuple-element.7, f32[2,4,64,128]{3,2,1,0:T(8,128)S(1)} %get-tuple-element.43, f32[2,4,64,128]{3,2,1,0:T(8,128)S(1)} %get-tuple-element.45, f32[6,4,64,128]{3,2,1,0:T(8,128)S(1)} %copy-done, f32[]{:T(128)} %bitcast.4, ...), kind=kLoop, calls=%fused_computation.305 | loop fusion | flops 786432 | bytes 1703952 | tf_op jit(solution)/shard_map/add | solution.py:72
  64.2 0.7 copy-done.3
  64.9 3.2 %fusion.73 = f32[4,64,128]{2,1,0:T(8,128)S(1)} fusion(f32[4,64,128]{2,1,0:T(8,128)S(1)} %get-tuple-element.10, f32[2,4,64,128]{3,2,1,0:T(8,128)S(1)} %get-tuple-element.44, f32[4,64,128]{2,1,0:T(8,128)S(1)} %get-tuple-element.8, f32[2,4,64,128]{3,2,1,0:T(8,128)S(1)} %get-tuple-element.43, f32[64,128]{1,0:T(8,128)S(1)} %copy-done.3, ...), kind=kLoop, calls=%fused_computation.161 | loop fusion | flops 688128 | bytes 950308 | tf_op jit(solution)/shard_map/add | solution.py:70
  68.1 0.1 fusion.8
  68.3 1.9 %collective-permute-start.6 = (f32[2,4,1,128]{3,2,1,0:T(1,128)S(1)}, f32[2,4,1,128]{3,2,1,0:T(1,128)S(1)}, u32[]{:S(2)}, u32[]{:S(2)}) collective-permute-start(f32[2,4,1,128]{3,2,1,0:T(1,128)S(1)} %pad_maximum_fusion.33), channel_id=1, source_target_pairs={{0,12},{4,0},{8,4},{12,8},{1,13},{5,1},{9,5},{13,9},{2,14},{6,2},{... | collective-permute-start | bytes 12296 | tf_op jit(solution)/shard_map/ppermute | solution.py:17
  70.3 5.8 %collective-permute-start.8 = (f32[2,1,64,128]{3,2,1,0:T(8,128)S(1)}, f32[2,1,64,128]{3,2,1,0:T(8,128)S(1)}, u32[]{:S(2)}, u32[]{:S(2)}) collective-permute-start(f32[2,1,64,128]{3,2,1,0:T(8,128)S(1)} %pad_maximum_fusion.30), channel_id=1, source_target_pairs={{16,0},{32,16},{48,32},{64,48},{80,64},{96,80},{112,96},{128,112},... | collective-permute-start | bytes 196616 | tf_op jit(solution)/shard_map/ppermute | solution.py:12
  76.0 3.6 %collective-permute-start.7 = (f32[2,4,64,1]{3,2,1,0:T(8,128)S(1)}, f32[2,4,64,1]{3,2,1,0:T(8,128)S(1)}, u32[]{:S(2)}, u32[]{:S(2)}) collective-permute-start(f32[2,4,64,1]{3,2,1,0:T(8,128)S(1)} %pad_maximum_fusion.11), channel_id=1, source_target_pairs={{0,3},{1,0},{2,1},{3,2},{4,7},{5,4},{6,5},{7,6},{8,11},{9,8},{10,9... | collective-permute-start | bytes 6152 | tf_op jit(solution)/shard_map/ppermute | solution.py:17
  79.7 3.4 %collective-permute-done.7 = f32[2,4,64,1]{3,2,1,0:T(8,128)S(1)} collective-permute-done((f32[2,4,64,1]{3,2,1,0:T(8,128)S(1)}, f32[2,4,64,1]{3,2,1,0:T(8,128)S(1)}, u32[]{:S(2)}, u32[]{:S(2)}) %collective-permute-start.7) | collective-permute-done | bytes 2080 | tf_op jit(solution)/shard_map/ppermute | solution.py:17
  83.1 0.2 fusion.66
  83.4 9.0 %collective-permute-start.11 = (f32[2,4,1,128]{3,2,1,0:T(1,128)S(1)}, f32[2,4,1,128]{3,2,1,0:T(1,128)S(1)}, u32[]{:S(2)}, u32[]{:S(2)}) collective-permute-start(f32[2,4,1,128]{3,2,1,0:T(1,128)S(1)} %fusion.204), channel_id=1, source_target_pairs={{0,4},{4,8},{8,12},{12,0},{1,5},{5,9},{9,13},{13,1},{2,6},{6,10},{... | collective-permute-start | bytes 12296 | tf_op jit(solution)/shard_map/ppermute | solution.py:17
  92.4 1.9 %collective-permute-start.10 = (f32[2,1,64,128]{3,2,1,0:T(8,128)S(1)}, f32[2,1,64,128]{3,2,1,0:T(8,128)S(1)}, u32[]{:S(2)}, u32[]{:S(2)}) collective-permute-start(f32[2,1,64,128]{3,2,1,0:T(8,128)S(1)} %fusion.200), channel_id=1, source_target_pairs={{0,16},{16,32},{32,48},{48,64},{64,80},{80,96},{96,112},{112,128},... | collective-permute-start | bytes 196616 | tf_op jit(solution)/shard_map/ppermute | solution.py:12
  94.3 0.1 fusion.2
  94.4 1.9 %collective-permute-start.9 = (f32[2,4,64,1]{3,2,1,0:T(8,128)S(1)}, f32[2,4,64,1]{3,2,1,0:T(8,128)S(1)}, u32[]{:S(2)}, u32[]{:S(2)}) collective-permute-start(f32[2,4,64,1]{3,2,1,0:T(8,128)S(1)} %fusion.2), channel_id=1, source_target_pairs={{0,1},{1,2},{2,3},{3,0},{4,5},{5,6},{6,7},{7,4},{8,9},{9,10},{10,1... | collective-permute-start | bytes 6152 | tf_op jit(solution)/shard_map/ppermute | solution.py:17
  96.4 6.8 %collective-permute-done.9 = f32[2,4,64,1]{3,2,1,0:T(8,128)S(1)} collective-permute-done((f32[2,4,64,1]{3,2,1,0:T(8,128)S(1)}, f32[2,4,64,1]{3,2,1,0:T(8,128)S(1)}, u32[]{:S(2)}, u32[]{:S(2)}) %collective-permute-start.9) | collective-permute-done | bytes 2080 | tf_op jit(solution)/shard_map/ppermute | solution.py:17
  103.1 0.1 fusion.17
  103.3 2.6 %fusion.153 = f32[4,64,128]{2,1,0:T(8,128)S(1)} fusion(f32[4,64,128]{2,1,0:T(8,128)S(1)} %get-tuple-element.9, f32[4,64,128]{2,1,0:T(8,128)S(1)} %get-tuple-element.28, f32[2,4,64,128]{3,2,1,0:T(8,128)S(1)} %get-tuple-element.41, f32[4,64,128]{2,1,0:T(8,128)S(1)} %get-tuple-element.29, f32[2,4,64,128]{3,2,1,0:T(8,128)S(1)} %get-tuple-element.42, ...), kind=kLoop, calls=%fused_computation.272 | loop fusion | flops 557056 | bytes 917520 | tf_op jit(solution)/shard_map/add | solution.py:72
  105.9 3.3 %fusion.74 = (f32[4,64,128]{2,1,0:T(8,128)S(1)}, f32[4,64,128]{2,1,0:T(8,128)S(1)}) fusion(f32[4,64,128]{2,1,0:T(8,128)S(1)} %fusion.73, f32[4,64,128]{2,1,0:T(8,128)S(1)} %get-tuple-element.29, f32[2,4,64,128]{3,2,1,0:T(8,128)S(1)} %get-tuple-element.40, f32[4,64,128]{2,1,0:T(8,128)S(1)} %get-tuple-element.27, f32[2,4,64,128]{3,2,1,0:T(8,128)S(1)} %get-tuple-element.41, ...), kind=kLoop, calls=%fused_computation.162 | loop fusion | flops 851968 | bytes 1605668 | tf_op jit(solution)/shard_map/add | solution.py:70
  109.2 0.1 fusion.6
  109.4 1.9 %collective-permute-start.12 = (f32[2,4,1,128]{3,2,1,0:T(1,128)S(1)}, f32[2,4,1,128]{3,2,1,0:T(1,128)S(1)}, u32[]{:S(2)}, u32[]{:S(2)}) collective-permute-start(f32[2,4,1,128]{3,2,1,0:T(1,128)S(1)} %pad_maximum_fusion.32), channel_id=1, source_target_pairs={{0,12},{4,0},{8,4},{12,8},{1,13},{5,1},{9,5},{13,9},{2,14},{6,2},{... | collective-permute-start | bytes 12296 | tf_op jit(solution)/shard_map/ppermute | solution.py:17
  111.3 5.8 %collective-permute-start.14 = (f32[2,1,64,128]{3,2,1,0:T(8,128)S(1)}, f32[2,1,64,128]{3,2,1,0:T(8,128)S(1)}, u32[]{:S(2)}, u32[]{:S(2)}) collective-permute-start(f32[2,1,64,128]{3,2,1,0:T(8,128)S(1)} %pad_maximum_fusion.29), channel_id=1, source_target_pairs={{16,0},{32,16},{48,32},{64,48},{80,64},{96,80},{112,96},{128,112},... | collective-permute-start | bytes 196616 | tf_op jit(solution)/shard_map/ppermute | solution.py:12
  117.0 3.6 %collective-permute-start.13 = (f32[2,4,64,1]{3,2,1,0:T(8,128)S(1)}, f32[2,4,64,1]{3,2,1,0:T(8,128)S(1)}, u32[]{:S(2)}, u32[]{:S(2)}) collective-permute-start(f32[2,4,64,1]{3,2,1,0:T(8,128)S(1)} %pad_maximum_fusion.7), channel_id=1, source_target_pairs={{0,3},{1,0},{2,1},{3,2},{4,7},{5,4},{6,5},{7,6},{8,11},{9,8},{10,9... | collective-permute-start | bytes 6152 | tf_op jit(solution)/shard_map/ppermute | solution.py:17
  120.7 3.4 %collective-permute-done.13 = f32[2,4,64,1]{3,2,1,0:T(8,128)S(1)} collective-permute-done((f32[2,4,64,1]{3,2,1,0:T(8,128)S(1)}, f32[2,4,64,1]{3,2,1,0:T(8,128)S(1)}, u32[]{:S(2)}, u32[]{:S(2)}) %collective-permute-start.13) | collective-permute-done | bytes 2080 | tf_op jit(solution)/shard_map/ppermute | solution.py:17
  124.2 0.2 fusion.51
  124.4 9.0 %collective-permute-start.17 = (f32[2,4,1,128]{3,2,1,0:T(1,128)S(1)}, f32[2,4,1,128]{3,2,1,0:T(1,128)S(1)}, u32[]{:S(2)}, u32[]{:S(2)}) collective-permute-start(f32[2,4,1,128]{3,2,1,0:T(1,128)S(1)} %fusion.203), channel_id=1, source_target_pairs={{0,4},{4,8},{8,12},{12,0},{1,5},{5,9},{9,13},{13,1},{2,6},{6,10},{... | collective-permute-start | bytes 12296 | tf_op jit(solution)/shard_map/ppermute | solution.py:17
  133.4 1.9 %collective-permute-start.16 = (f32[2,1,64,128]{3,2,1,0:T(8,128)S(1)}, f32[2,1,64,128]{3,2,1,0:T(8,128)S(1)}, u32[]{:S(2)}, u32[]{:S(2)}) collective-permute-start(f32[2,1,64,128]{3,2,1,0:T(8,128)S(1)} %fusion.199), channel_id=1, source_target_pairs={{0,16},{16,32},{32,48},{48,64},{64,80},{80,96},{96,112},{112,128},... | collective-permute-start | bytes 196616 | tf_op jit(solution)/shard_map/ppermute | solution.py:12
  135.4 1.9 %collective-permute-start.15 = (f32[2,4,64,1]{3,2,1,0:T(8,128)S(1)}, f32[2,4,64,1]{3,2,1,0:T(8,128)S(1)}, u32[]{:S(2)}, u32[]{:S(2)}) collective-permute-start(f32[2,4,64,1]{3,2,1,0:T(8,128)S(1)} %fusion.1), channel_id=1, source_target_pairs={{0,1},{1,2},{2,3},{3,0},{4,5},{5,6},{6,7},{7,4},{8,9},{9,10},{10,1... | collective-permute-start | bytes 6152 | tf_op jit(solution)/shard_map/ppermute | solution.py:17
  137.4 7.4 %collective-permute-done.15 = f32[2,4,64,1]{3,2,1,0:T(8,128)S(1)} collective-permute-done((f32[2,4,64,1]{3,2,1,0:T(8,128)S(1)}, f32[2,4,64,1]{3,2,1,0:T(8,128)S(1)}, u32[]{:S(2)}, u32[]{:S(2)}) %collective-permute-start.15) | collective-permute-done | bytes 2080 | tf_op jit(solution)/shard_map/ppermute | solution.py:17
  144.8 0.1 fusion.14
  145.0 2.6 %fusion.129 = f32[4,64,128]{2,1,0:T(8,128)S(1)} fusion(f32[4,64,128]{2,1,0:T(8,128)S(1)} %fusion.153, f32[4,64,128]{2,1,0:T(8,128)S(1)} %get-tuple-element.25, f32[2,4,64,128]{3,2,1,0:T(8,128)S(1)} %get-tuple-element.38, f32[4,64,128]{2,1,0:T(8,128)S(1)} %get-tuple-element.26, f32[2,4,64,128]{3,2,1,0:T(8,128)S(1)} %get-tuple-element.39, f32[]{:T(128)} %bitcast.4, ...), kind=kLoop, calls=%fused_computation.239 | loop fusion | flops 557056 | bytes 917520 | tf_op jit(solution)/shard_map/add | solution.py:72
  147.6 3.3 %fusion.75 = (f32[4,64,128]{2,1,0:T(8,128)S(1)}, f32[4,64,128]{2,1,0:T(8,128)S(1)}) fusion(f32[4,64,128]{2,1,0:T(8,128)S(1)} %get-tuple-element.32, f32[4,64,128]{2,1,0:T(8,128)S(1)} %get-tuple-element.26, f32[2,4,64,128]{3,2,1,0:T(8,128)S(1)} %get-tuple-element.37, f32[4,64,128]{2,1,0:T(8,128)S(1)} %get-tuple-element.24, ...), kind=kLoop, calls=%fused_computation.163 | loop fusion | flops 851968 | bytes 1605668 | tf_op jit(solution)/shard_map/add | solution.py:70
  150.9 0.1 fusion.4
  151.1 1.9 %collective-permute-start.18 = (f32[2,4,1,128]{3,2,1,0:T(1,128)S(1)}, f32[2,4,1,128]{3,2,1,0:T(1,128)S(1)}, u32[]{:S(2)}, u32[]{:S(2)}) collective-permute-start(f32[2,4,1,128]{3,2,1,0:T(1,128)S(1)} %pad_maximum_fusion.31), channel_id=1, source_target_pairs={{0,12},{4,0},{8,4},{12,8},{1,13},{5,1},{9,5},{13,9},{2,14},{6,2},{... | collective-permute-start | bytes 12296 | tf_op jit(solution)/shard_map/ppermute | solution.py:17
  153.0 5.8 %collective-permute-start.20 = (f32[2,1,64,128]{3,2,1,0:T(8,128)S(1)}, f32[2,1,64,128]{3,2,1,0:T(8,128)S(1)}, u32[]{:S(2)}, u32[]{:S(2)}) collective-permute-start(f32[2,1,64,128]{3,2,1,0:T(8,128)S(1)} %pad_maximum_fusion.28), channel_id=1, source_target_pairs={{16,0},{32,16},{48,32},{64,48},{80,64},{96,80},{112,96},{128,112},... | collective-permute-start | bytes 196616 | tf_op jit(solution)/shard_map/ppermute | solution.py:12
  158.7 3.6 %collective-permute-start.19 = (f32[2,4,64,1]{3,2,1,0:T(8,128)S(1)}, f32[2,4,64,1]{3,2,1,0:T(8,128)S(1)}, u32[]{:S(2)}, u32[]{:S(2)}) collective-permute-start(f32[2,4,64,1]{3,2,1,0:T(8,128)S(1)} %pad_maximum_fusion.3), channel_id=1, source_target_pairs={{0,3},{1,0},{2,1},{3,2},{4,7},{5,4},{6,5},{7,6},{8,11},{9,8},{10,9... | collective-permute-start | bytes 6152 | tf_op jit(solution)/shard_map/ppermute | solution.py:17
  162.4 3.4 %collective-permute-done.19 = f32[2,4,64,1]{3,2,1,0:T(8,128)S(1)} collective-permute-done((f32[2,4,64,1]{3,2,1,0:T(8,128)S(1)}, f32[2,4,64,1]{3,2,1,0:T(8,128)S(1)}, u32[]{:S(2)}, u32[]{:S(2)}) %collective-permute-start.19) | collective-permute-done | bytes 2080 | tf_op jit(solution)/shard_map/ppermute | solution.py:17
  165.9 0.2 fusion.36
  166.1 0.1 fusion
  166.2 9.1 %collective-permute-start.23 = (f32[2,4,1,128]{3,2,1,0:T(1,128)S(1)}, f32[2,4,1,128]{3,2,1,0:T(1,128)S(1)}, u32[]{:S(2)}, u32[]{:S(2)}) collective-permute-start(f32[2,4,1,128]{3,2,1,0:T(1,128)S(1)} %fusion.202), channel_id=1, source_target_pairs={{0,4},{4,8},{8,12},{12,0},{1,5},{5,9},{9,13},{13,1},{2,6},{6,10},{... | collective-permute-start | bytes 12296 | tf_op jit(solution)/shard_map/ppermute | solution.py:17
  175.4 1.9 %collective-permute-start.22 = (f32[2,1,64,128]{3,2,1,0:T(8,128)S(1)}, f32[2,1,64,128]{3,2,1,0:T(8,128)S(1)}, u32[]{:S(2)}, u32[]{:S(2)}) collective-permute-start(f32[2,1,64,128]{3,2,1,0:T(8,128)S(1)} %fusion.198), channel_id=1, source_target_pairs={{0,16},{16,32},{32,48},{48,64},{64,80},{80,96},{96,112},{112,128},... | collective-permute-start | bytes 196616 | tf_op jit(solution)/shard_map/ppermute | solution.py:12
  177.3 1.9 %collective-permute-start.21 = (f32[2,4,64,1]{3,2,1,0:T(8,128)S(1)}, f32[2,4,64,1]{3,2,1,0:T(8,128)S(1)}, u32[]{:S(2)}, u32[]{:S(2)}) collective-permute-start(f32[2,4,64,1]{3,2,1,0:T(8,128)S(1)} %fusion), channel_id=1, source_target_pairs={{0,1},{1,2},{2,3},{3,0},{4,5},{5,6},{6,7},{7,4},{8,9},{9,10},{10,1... | collective-permute-start | bytes 6152 | tf_op jit(solution)/shard_map/ppermute | solution.py:17
  179.2 0.2 slice_convert_fusion.3
  179.4 6.6 %collective-permute-done.21 = f32[2,4,64,1]{3,2,1,0:T(8,128)S(1)} collective-permute-done((f32[2,4,64,1]{3,2,1,0:T(8,128)S(1)}, f32[2,4,64,1]{3,2,1,0:T(8,128)S(1)}, u32[]{:S(2)}, u32[]{:S(2)}) %collective-permute-start.21) | collective-permute-done | bytes 2080 | tf_op jit(solution)/shard_map/ppermute | solution.py:17
  186.0 0.1 fusion.11
  186.1 4.2 %fusion.80 = (f32[4,64,128]{2,1,0:T(8,128)}, f32[4,64,128]{2,1,0:T(8,128)S(1)}, f32[4,64,128]{2,1,0:T(8,128)S(1)}, f32[4,64,128]{2,1,0:T(8,128)S(1)}) fusion(f32[1,3,4,64,128]{4,3,2,1,0:T(8,128)S(1)} %get-tuple-element.16, f32[4,64,128]{2,1,0:T(8,128)S(1)} %fusion.129, f32[1,3,4,64,128]{4,3,2,1,0:T(8,128)S(1)} %get-tuple-element.17, ...), kind=kLoop, calls=%fused_computation.169 | loop fusion | flops 1867776 | bytes 4620324 | tf_op jit(solution)/shard_map/jit(_where)/select_n | solution.py:114
  190.4 0.9 copy-done.4
  (57 shorter events, 0.6 us)
Async XLA Ops:
  0.6 27.6 %copy-start = (f32[6,4,64,128]{3,2,1,0:T(8,128)S(1)}, f32[6,4,64,128]{3,2,1,0:T(8,128)}, u32[]{:S(2)}) copy-start(f32[6,4,64,128]{3,2,1,0:T(8,128)} %param.7) | copy-start | bytes 2359300
  1.5 26.7 %collective-permute-start = (f32[2,4,1,128]{3,2,1,0:T(1,128)S(1)}, f32[2,4,1,128]{3,2,1,0:T(1,128)S(1)}, u32[]{:S(2)}, u32[]{:S(2)}) collective-permute-start(f32[2,4,1,128]{3,2,1,0:T(1,128)S(1)} %slice.411), channel_id=1, source_target_pairs={{0,12},{4,0},{8,4},{12,8},{1,13},{5,1},{9,5},{13,9},{2,14},{6,2},{... | collective-permute-start | bytes 12296 | tf_op jit(solution)/shard_map/ppermute | solution.py:17
  4.9 23.3 %collective-permute-start.2 = (f32[2,1,64,128]{3,2,1,0:T(8,128)S(1)}, f32[2,1,64,128]{3,2,1,0:T(8,128)S(1)}, u32[]{:S(2)}, u32[]{:S(2)}) collective-permute-start(f32[2,1,64,128]{3,2,1,0:T(8,128)S(1)} %slice.421), channel_id=1, source_target_pairs={{16,0},{32,16},{48,32},{64,48},{80,64},{96,80},{112,96},{128,112},... | collective-permute-start | bytes 196616 | tf_op jit(solution)/shard_map/ppermute | solution.py:12
  28.3 7.7 %collective-permute-start.1 = (f32[2,4,64,1]{3,2,1,0:T(8,128)S(1)}, f32[2,4,64,1]{3,2,1,0:T(8,128)S(1)}, u32[]{:S(2)}, u32[]{:S(2)}) collective-permute-start(f32[2,4,64,1]{3,2,1,0:T(8,128)S(1)} %pad_maximum_fusion.15), channel_id=1, source_target_pairs={{0,3},{1,0},{2,1},{3,2},{4,7},{5,4},{6,5},{7,6},{8,11},{9,8},{10,9... | collective-permute-start | bytes 6152 | tf_op jit(solution)/shard_map/ppermute | solution.py:17
  36.3 22.3 %collective-permute-start.5 = (f32[2,4,1,128]{3,2,1,0:T(1,128)S(1)}, f32[2,4,1,128]{3,2,1,0:T(1,128)S(1)}, u32[]{:S(2)}, u32[]{:S(2)}) collective-permute-start(f32[2,4,1,128]{3,2,1,0:T(1,128)S(1)} %fusion.205), channel_id=1, source_target_pairs={{0,4},{4,8},{8,12},{12,0},{1,5},{5,9},{9,13},{13,1},{2,6},{6,10},{... | collective-permute-start | bytes 12296 | tf_op jit(solution)/shard_map/ppermute | solution.py:17
  46.9 11.8 %collective-permute-start.4 = (f32[2,1,64,128]{3,2,1,0:T(8,128)S(1)}, f32[2,1,64,128]{3,2,1,0:T(8,128)S(1)}, u32[]{:S(2)}, u32[]{:S(2)}) collective-permute-start(f32[2,1,64,128]{3,2,1,0:T(8,128)S(1)} %fusion.201), channel_id=1, source_target_pairs={{0,16},{16,32},{32,48},{48,64},{64,80},{80,96},{96,112},{112,128},... | collective-permute-start | bytes 196616 | tf_op jit(solution)/shard_map/ppermute | solution.py:12
  48.8 9.8 %collective-permute-start.3 = (f32[2,4,64,1]{3,2,1,0:T(8,128)S(1)}, f32[2,4,64,1]{3,2,1,0:T(8,128)S(1)}, u32[]{:S(2)}, u32[]{:S(2)}) collective-permute-start(f32[2,4,64,1]{3,2,1,0:T(8,128)S(1)} %fusion.3), channel_id=1, source_target_pairs={{0,1},{1,2},{2,3},{3,0},{4,5},{5,6},{6,7},{7,4},{8,9},{9,10},{10,1... | collective-permute-start | bytes 6152 | tf_op jit(solution)/shard_map/ppermute | solution.py:17
  51.7 7.1 %copy-start.1 = (s32[4,64,128]{2,1,0:T(8,128)S(1)}, s32[4,64,128]{2,1,0:T(8,128)}, u32[]{:S(2)}) copy-start(s32[4,64,128]{2,1,0:T(8,128)} %param.8) | copy-start | bytes 393220
  64.1 0.8 copy-start.3
  68.3 14.8 %collective-permute-start.6 = (f32[2,4,1,128]{3,2,1,0:T(1,128)S(1)}, f32[2,4,1,128]{3,2,1,0:T(1,128)S(1)}, u32[]{:S(2)}, u32[]{:S(2)}) collective-permute-start(f32[2,4,1,128]{3,2,1,0:T(1,128)S(1)} %pad_maximum_fusion.33), channel_id=1, source_target_pairs={{0,12},{4,0},{8,4},{12,8},{1,13},{5,1},{9,5},{13,9},{2,14},{6,2},{... | collective-permute-start | bytes 12296 | tf_op jit(solution)/shard_map/ppermute | solution.py:17
  70.3 12.9 %collective-permute-start.8 = (f32[2,1,64,128]{3,2,1,0:T(8,128)S(1)}, f32[2,1,64,128]{3,2,1,0:T(8,128)S(1)}, u32[]{:S(2)}, u32[]{:S(2)}) collective-permute-start(f32[2,1,64,128]{3,2,1,0:T(8,128)S(1)} %pad_maximum_fusion.30), channel_id=1, source_target_pairs={{16,0},{32,16},{48,32},{64,48},{80,64},{96,80},{112,96},{128,112},... | collective-permute-start | bytes 196616 | tf_op jit(solution)/shard_map/ppermute | solution.py:12
  76.0 7.1 %collective-permute-start.7 = (f32[2,4,64,1]{3,2,1,0:T(8,128)S(1)}, f32[2,4,64,1]{3,2,1,0:T(8,128)S(1)}, u32[]{:S(2)}, u32[]{:S(2)}) collective-permute-start(f32[2,4,64,1]{3,2,1,0:T(8,128)S(1)} %pad_maximum_fusion.11), channel_id=1, source_target_pairs={{0,3},{1,0},{2,1},{3,2},{4,7},{5,4},{6,5},{7,6},{8,11},{9,8},{10,9... | collective-permute-start | bytes 6152 | tf_op jit(solution)/shard_map/ppermute | solution.py:17
  83.4 19.8 %collective-permute-start.11 = (f32[2,4,1,128]{3,2,1,0:T(1,128)S(1)}, f32[2,4,1,128]{3,2,1,0:T(1,128)S(1)}, u32[]{:S(2)}, u32[]{:S(2)}) collective-permute-start(f32[2,4,1,128]{3,2,1,0:T(1,128)S(1)} %fusion.204), channel_id=1, source_target_pairs={{0,4},{4,8},{8,12},{12,0},{1,5},{5,9},{9,13},{13,1},{2,6},{6,10},{... | collective-permute-start | bytes 12296 | tf_op jit(solution)/shard_map/ppermute | solution.py:17
  92.4 10.8 %collective-permute-start.10 = (f32[2,1,64,128]{3,2,1,0:T(8,128)S(1)}, f32[2,1,64,128]{3,2,1,0:T(8,128)S(1)}, u32[]{:S(2)}, u32[]{:S(2)}) collective-permute-start(f32[2,1,64,128]{3,2,1,0:T(8,128)S(1)} %fusion.200), channel_id=1, source_target_pairs={{0,16},{16,32},{32,48},{48,64},{64,80},{80,96},{96,112},{112,128},... | collective-permute-start | bytes 196616 | tf_op jit(solution)/shard_map/ppermute | solution.py:12
  94.4 8.7 %collective-permute-start.9 = (f32[2,4,64,1]{3,2,1,0:T(8,128)S(1)}, f32[2,4,64,1]{3,2,1,0:T(8,128)S(1)}, u32[]{:S(2)}, u32[]{:S(2)}) collective-permute-start(f32[2,4,64,1]{3,2,1,0:T(8,128)S(1)} %fusion.2), channel_id=1, source_target_pairs={{0,1},{1,2},{2,3},{3,0},{4,5},{5,6},{6,7},{7,4},{8,9},{9,10},{10,1... | collective-permute-start | bytes 6152 | tf_op jit(solution)/shard_map/ppermute | solution.py:17
  109.4 14.8 %collective-permute-start.12 = (f32[2,4,1,128]{3,2,1,0:T(1,128)S(1)}, f32[2,4,1,128]{3,2,1,0:T(1,128)S(1)}, u32[]{:S(2)}, u32[]{:S(2)}) collective-permute-start(f32[2,4,1,128]{3,2,1,0:T(1,128)S(1)} %pad_maximum_fusion.32), channel_id=1, source_target_pairs={{0,12},{4,0},{8,4},{12,8},{1,13},{5,1},{9,5},{13,9},{2,14},{6,2},{... | collective-permute-start | bytes 12296 | tf_op jit(solution)/shard_map/ppermute | solution.py:17
  111.3 12.9 %collective-permute-start.14 = (f32[2,1,64,128]{3,2,1,0:T(8,128)S(1)}, f32[2,1,64,128]{3,2,1,0:T(8,128)S(1)}, u32[]{:S(2)}, u32[]{:S(2)}) collective-permute-start(f32[2,1,64,128]{3,2,1,0:T(8,128)S(1)} %pad_maximum_fusion.29), channel_id=1, source_target_pairs={{16,0},{32,16},{48,32},{64,48},{80,64},{96,80},{112,96},{128,112},... | collective-permute-start | bytes 196616 | tf_op jit(solution)/shard_map/ppermute | solution.py:12
  117.0 7.1 %collective-permute-start.13 = (f32[2,4,64,1]{3,2,1,0:T(8,128)S(1)}, f32[2,4,64,1]{3,2,1,0:T(8,128)S(1)}, u32[]{:S(2)}, u32[]{:S(2)}) collective-permute-start(f32[2,4,64,1]{3,2,1,0:T(8,128)S(1)} %pad_maximum_fusion.7), channel_id=1, source_target_pairs={{0,3},{1,0},{2,1},{3,2},{4,7},{5,4},{6,5},{7,6},{8,11},{9,8},{10,9... | collective-permute-start | bytes 6152 | tf_op jit(solution)/shard_map/ppermute | solution.py:17
  124.4 20.4 %collective-permute-start.17 = (f32[2,4,1,128]{3,2,1,0:T(1,128)S(1)}, f32[2,4,1,128]{3,2,1,0:T(1,128)S(1)}, u32[]{:S(2)}, u32[]{:S(2)}) collective-permute-start(f32[2,4,1,128]{3,2,1,0:T(1,128)S(1)} %fusion.203), channel_id=1, source_target_pairs={{0,4},{4,8},{8,12},{12,0},{1,5},{5,9},{9,13},{13,1},{2,6},{6,10},{... | collective-permute-start | bytes 12296 | tf_op jit(solution)/shard_map/ppermute | solution.py:17
  133.4 11.4 %collective-permute-start.16 = (f32[2,1,64,128]{3,2,1,0:T(8,128)S(1)}, f32[2,1,64,128]{3,2,1,0:T(8,128)S(1)}, u32[]{:S(2)}, u32[]{:S(2)}) collective-permute-start(f32[2,1,64,128]{3,2,1,0:T(8,128)S(1)} %fusion.199), channel_id=1, source_target_pairs={{0,16},{16,32},{32,48},{48,64},{64,80},{80,96},{96,112},{112,128},... | collective-permute-start | bytes 196616 | tf_op jit(solution)/shard_map/ppermute | solution.py:12
  135.4 9.4 %collective-permute-start.15 = (f32[2,4,64,1]{3,2,1,0:T(8,128)S(1)}, f32[2,4,64,1]{3,2,1,0:T(8,128)S(1)}, u32[]{:S(2)}, u32[]{:S(2)}) collective-permute-start(f32[2,4,64,1]{3,2,1,0:T(8,128)S(1)} %fusion.1), channel_id=1, source_target_pairs={{0,1},{1,2},{2,3},{3,0},{4,5},{5,6},{6,7},{7,4},{8,9},{9,10},{10,1... | collective-permute-start | bytes 6152 | tf_op jit(solution)/shard_map/ppermute | solution.py:17
  151.1 14.8 %collective-permute-start.18 = (f32[2,4,1,128]{3,2,1,0:T(1,128)S(1)}, f32[2,4,1,128]{3,2,1,0:T(1,128)S(1)}, u32[]{:S(2)}, u32[]{:S(2)}) collective-permute-start(f32[2,4,1,128]{3,2,1,0:T(1,128)S(1)} %pad_maximum_fusion.31), channel_id=1, source_target_pairs={{0,12},{4,0},{8,4},{12,8},{1,13},{5,1},{9,5},{13,9},{2,14},{6,2},{... | collective-permute-start | bytes 12296 | tf_op jit(solution)/shard_map/ppermute | solution.py:17
  153.0 12.9 %collective-permute-start.20 = (f32[2,1,64,128]{3,2,1,0:T(8,128)S(1)}, f32[2,1,64,128]{3,2,1,0:T(8,128)S(1)}, u32[]{:S(2)}, u32[]{:S(2)}) collective-permute-start(f32[2,1,64,128]{3,2,1,0:T(8,128)S(1)} %pad_maximum_fusion.28), channel_id=1, source_target_pairs={{16,0},{32,16},{48,32},{64,48},{80,64},{96,80},{112,96},{128,112},... | collective-permute-start | bytes 196616 | tf_op jit(solution)/shard_map/ppermute | solution.py:12
  158.7 7.1 %collective-permute-start.19 = (f32[2,4,64,1]{3,2,1,0:T(8,128)S(1)}, f32[2,4,64,1]{3,2,1,0:T(8,128)S(1)}, u32[]{:S(2)}, u32[]{:S(2)}) collective-permute-start(f32[2,4,64,1]{3,2,1,0:T(8,128)S(1)} %pad_maximum_fusion.3), channel_id=1, source_target_pairs={{0,3},{1,0},{2,1},{3,2},{4,7},{5,4},{6,5},{7,6},{8,11},{9,8},{10,9... | collective-permute-start | bytes 6152 | tf_op jit(solution)/shard_map/ppermute | solution.py:17
  166.1 13.2 %copy-start.2 = (bf16[4,3,4,64,128]{4,3,2,1,0:T(8,128)(2,1)S(1)}, bf16[4,3,4,64,128]{4,3,2,1,0:T(8,128)(2,1)}, u32[]{:S(2)}) copy-start(bf16[4,3,4,64,128]{4,3,2,1,0:T(8,128)(2,1)} %param.13) | copy-start | bytes 2359300
  166.2 19.7 %collective-permute-start.23 = (f32[2,4,1,128]{3,2,1,0:T(1,128)S(1)}, f32[2,4,1,128]{3,2,1,0:T(1,128)S(1)}, u32[]{:S(2)}, u32[]{:S(2)}) collective-permute-start(f32[2,4,1,128]{3,2,1,0:T(1,128)S(1)} %fusion.202), channel_id=1, source_target_pairs={{0,4},{4,8},{8,12},{12,0},{1,5},{5,9},{9,13},{13,1},{2,6},{6,10},{... | collective-permute-start | bytes 12296 | tf_op jit(solution)/shard_map/ppermute | solution.py:17
  175.4 10.6 %collective-permute-start.22 = (f32[2,1,64,128]{3,2,1,0:T(8,128)S(1)}, f32[2,1,64,128]{3,2,1,0:T(8,128)S(1)}, u32[]{:S(2)}, u32[]{:S(2)}) collective-permute-start(f32[2,1,64,128]{3,2,1,0:T(8,128)S(1)} %fusion.198), channel_id=1, source_target_pairs={{0,16},{16,32},{32,48},{48,64},{64,80},{80,96},{96,112},{112,128},... | collective-permute-start | bytes 196616 | tf_op jit(solution)/shard_map/ppermute | solution.py:12
  177.3 8.7 %collective-permute-start.21 = (f32[2,4,64,1]{3,2,1,0:T(8,128)S(1)}, f32[2,4,64,1]{3,2,1,0:T(8,128)S(1)}, u32[]{:S(2)}, u32[]{:S(2)}) collective-permute-start(f32[2,4,64,1]{3,2,1,0:T(8,128)S(1)} %fusion), channel_id=1, source_target_pairs={{0,1},{1,2},{2,3},{3,0},{4,5},{5,6},{6,7},{7,4},{8,9},{9,10},{10,1... | collective-permute-start | bytes 6152 | tf_op jit(solution)/shard_map/ppermute | solution.py:17
  190.4 0.9 copy-start.4
where the time goes:
time: 193 us; the launch traced here: 191 us
  starting transfers between devices  113 us (59%)
  waiting for transfers between devices  41.3 us (21%)
  other arithmetic  27.2 us (14%)
  local copies, waits for them, and re-layouts  8.21 us (4%)
  between operations  1.94 us (1%)
    ppermute x16, starting transfers between devices, passed_along(): lax.ppermute(array, axis, [(i, (i + by) % length) for i in range(length)])  69.9 us
    ppermute x8, starting transfers between devices, from_behind(): return lax.ppermute(block, axis, route)  42.8 us
    ppermute x16, waiting for transfers between devices, passed_along(): lax.ppermute(array, axis, [(i, (i + by) % length) for i in range(length)])  41.3 us
    add x3, other arithmetic, yee_step(): new_x = elec_x + coef * back_x + coef * amplitude * source  9.75 us
    add x3, other arithmetic, yee_step(): new_z = elec_z + coef * back_z  7.78 us
    select_n x1, other arithmetic, on_device(): eps_grad = jnp.where(material >= 2, -grad, 0.0)  4.16 us
  transfers between devices with their start and end apart: 24, of which 8 were waited for; matrix products, arithmetic and copies ran while one was open for 3% of the time, Pallas kernels for 0%

commit v1 on v0

v1 whole, which is shorter than its diff:
```python
import functools

import jax
import jax.numpy as jnp
from jax import lax
from jax.experimental import pallas as pl
from jax.experimental.pallas import tpu as pltpu
from jax.sharding import PartitionSpec as P

COURANT = 0.5
MESH = pl.DeviceIdType.MESH
AXES = ("gz", "gx", "gy")


def around(axis, by):
    size = lax.axis_size(axis)
    return lax.rem(lax.axis_index(axis) + by + size, size)


def half_copies(field, row, packed, zghost, xghost, yghost, send, recv, slot, by):
    pieces = (
        (field.at[pl.ds(row, 2), 0 if by < 0 else field.shape[1] - 1], zghost.at[slot], "gz"),
        (
            field.at[
                pl.ds(row + 1, 2), :, pl.ds(0 if by < 0 else field.shape[2] - 8, 8)
            ],
            xghost.at[slot],
            "gx",
        ),
        (packed.at[slot], yghost.at[slot], "gy"),
    )
    return [
        pltpu.make_async_remote_copy(
            src_ref=src,
            dst_ref=dst,
            send_sem=send.at[slot, k],
            recv_sem=recv.at[slot, k],
            device_id={axis: around(axis, by)},
            device_id_type=MESH,
        )
        for k, (src, dst, axis) in enumerate(pieces)
    ]


def kernel(
    steps,
    eps_ref,
    plane_ref,
    wave_ref,
    fields_ref,
    material_ref,
    profile_ref,
    forward_ref,
    out_ref,
    grad_ref,
    coef_ref,
    packed,
    zghost,
    xghost,
    yghost,
    send,
    recv,
):
    _, depth, rows, lanes = fields_ref.shape
    gz, last = lax.axis_index("gz"), lax.axis_size("gz") - 1

    barrier = pltpu.get_barrier_semaphore()
    for axis in AXES:
        for by in (1, -1):
            pl.semaphore_signal(
                barrier, inc=1, device_id={axis: around(axis, by)}, device_id_type=MESH
            )

    for p in range(depth):
        kinds = material_ref[p]
        permit = jnp.full(kinds.shape, eps_ref[0], jnp.float32)
        for which in range(1, eps_ref.shape[0]):
            permit = jnp.where(kinds == which, eps_ref[which], permit)
        coef_ref[p] = COURANT / permit

    lane = lax.broadcasted_iota(jnp.int32, (rows, lanes), 1)
    row = lax.broadcasted_iota(jnp.int32, (rows, lanes), 0)

    def pack(ref, names, slot, shift):
        out = jnp.zeros((rows, lanes), jnp.float32)
        q = 0
        for c in names:
            for p in range(depth):
                v = ref[c, p]
                turn = (q + shift) % lanes
                out = jnp.where(lane == q, pltpu.roll(v, turn, 1) if turn else v, out)
                q += 1
        packed[slot] = out

    def start(copies, by):
        edge = 0 if by < 0 else last

        @pl.when(gz != edge)
        def _():
            copies[0].start()

        copies[1].start()
        copies[2].start()

    def finish(copies, by, slot):
        edge = last if by < 0 else 0

        @pl.when(gz != edge)
        def _():
            copies[0].wait_recv()

        @pl.when(gz == edge)
        def _():
            zghost[slot] = jnp.zeros(zghost.shape[1:], jnp.float32)

        copies[1].wait_recv()
        copies[2].wait_recv()

    def sent(copies, by):
        edge = 0 if by < 0 else last

        @pl.when(gz != edge)
        def _():
            copies[0].wait_send()

        copies[1].wait_send()
        copies[2].wait_send()

    pack(fields_ref, (0, 2), 0, 0)
    pl.semaphore_wait(barrier, 2 * len(AXES))
    pending = half_copies(fields_ref, 0, packed, zghost, xghost, yghost, send, recv, 0, -1)
    start(pending, -1)

    for t in range(steps):
        now = fields_ref if t == 0 else out_ref
        slot = 2 * t
        finish(pending, -1, slot)

        def after_x(c, p):
            v = now[c, p]
            border = jnp.broadcast_to(xghost[slot, c - 1, p, 0:1], v.shape)
            return jnp.where(row == rows - 1, border, pltpu.roll(v, rows - 1, 0)) - v

        def after_y(c, p):
            v = now[c, p]
            q = p if c == 0 else depth + p
            border = pltpu.roll(yghost[slot], lanes - 1 - q, 1)
            return jnp.where(lane == lanes - 1, border, pltpu.roll(v, lanes - 1, 1)) - v

        def after_z(c, p):
            following = now[c, p + 1] if p + 1 < depth else zghost[slot, c]
            return following - now[c, p]

        for p in range(depth - 1, -1, -1):
            out_ref[3, p] = now[3, p] - COURANT * (after_y(2, p) - after_z(1, p))
            out_ref[4, p] = now[4, p] - COURANT * (after_z(0, p) - after_x(2, p))
            out_ref[5, p] = now[5, p] - COURANT * (after_x(1, p) - after_y(0, p))
        pack(out_ref, (3, 5), slot + 1, 1)
        copies = half_copies(
            out_ref, 3, packed, zghost, xghost, yghost, send, recv, slot + 1, 1
        )
        start(copies, 1)
        sent(pending, -1)
        finish(copies, 1, slot + 1)

        def before_x(c, p):
            v = out_ref[c, p]
            border = jnp.broadcast_to(xghost[slot + 1, c - 4, p, 7:8], v.shape)
            return v - jnp.where(row == 0, border, pltpu.roll(v, 1, 0))

        def before_y(c, p):
            v = out_ref[c, p]
            q = p if c == 3 else depth + p
            border = yghost[slot + 1]
            border = pltpu.roll(border, lanes - q, 1) if q else border
            return v - jnp.where(lane == 0, border, pltpu.roll(v, 1, 1))

        def before_z(c, p):
            previous = out_ref[c, p - 1] if p > 0 else zghost[slot + 1, c - 3]
            return out_ref[c, p] - previous

        amplitude = wave_ref[t]
        for p in range(depth):
            coef = coef_ref[p]
            here = (gz * depth + p == plane_ref[0]).astype(jnp.float32)
            pushed = (amplitude * here) * profile_ref[...]
            out_ref[0, p] = now[0, p] + coef * (before_y(5, p) - before_z(4, p) + pushed)
            out_ref[1, p] = now[1, p] + coef * (before_z(3, p) - before_x(5, p))
            out_ref[2, p] = now[2, p] + coef * (before_x(4, p) - before_y(3, p))
        sent(copies, 1)
        if t + 1 < steps:
            pack(out_ref, (0, 2), slot + 2, 0)
            pending = half_copies(
                out_ref, 0, packed, zghost, xghost, yghost, send, recv, slot + 2, -1
            )
            start(pending, -1)
        for p in range(depth):
            total = jnp.zeros((rows, lanes), jnp.float32) if t == 0 else grad_ref[p]
            for c in range(3):
                total = total + forward_ref[t, c, p].astype(jnp.float32) * out_ref[c, p]
            if t + 1 == steps:
                total = jnp.where(material_ref[p] >= 2, -total, 0.0)
            grad_ref[p] = total


def on_device(
    fields_in, material, material_eps, source_plane, source_wave, source_profile, forward_fields
):
    depth, rows, lanes = material.shape
    steps = source_wave.shape[0]
    slots = 2 * steps
    whole = pl.BlockSpec(memory_space=pltpu.VMEM)
    scalars = pl.BlockSpec(memory_space=pltpu.SMEM)
    return pl.pallas_call(
        functools.partial(kernel, steps),
        out_shape=(
            jax.ShapeDtypeStruct(fields_in.shape, jnp.float32),
            jax.ShapeDtypeStruct(material.shape, jnp.float32),
        ),
        in_specs=[scalars] * 3 + [whole] * 4,
        out_specs=(whole, whole),
        scratch_shapes=[
            pltpu.VMEM((depth, rows, lanes), jnp.float32),
            pltpu.VMEM((slots, rows, lanes), jnp.float32),
            pltpu.VMEM((slots, 2, rows, lanes), jnp.float32),
            pltpu.VMEM((slots, 2, depth, 8, lanes), jnp.float32),
            pltpu.VMEM((slots, rows, lanes), jnp.float32),
            pltpu.SemaphoreType.DMA((slots, 3)),
            pltpu.SemaphoreType.DMA((slots, 3)),
        ],
        compiler_params=pltpu.CompilerParams(
            collective_id=0, has_side_effects=True, vmem_limit_bytes=32 << 20
        ),
    )(
        material_eps,
        source_plane,
        source_wave,
        fields_in,
        material,
        source_profile,
        forward_fields,
    )


def solution(mesh):
    placed = (
        P(None, "gz", "gx", "gy"),
        P("gz", "gx", "gy"),
        P(),
        P(),
        P(),
        P("gx", "gy"),
        P(None, None, "gz", "gx", "gy"),
    )
    return jax.shard_map(
        on_device,
        mesh=mesh,
        in_specs=placed,
        out_specs=(P(None, "gz", "gx", "gy"), P("gz", "gx", "gy")),
        check_vma=False,
    )
```

time: 193 us -> 69.4 us (0.36)
  the two profiles are of different devices: /device:TPU:9 before, /device:TPU:1 now
where the time goes in v1:
time: 69.4 us; the launch traced here: 69.1 us
  Pallas kernels  62.2 us (90%)
  local copies, waits for them, and re-layouts  5.47 us (8%)
  between operations  1.35 us (2%)
    pallas_call x1, Pallas kernels, on_device(): pl.pallas_call(functools.partial(kernel, steps), out_shape=(jax.ShapeDtyp...  62.2 us
    unnamed x14, local copies, waits for them, and re-layouts  5.47 us

profile of v1, /device:TPU:1, one launch (start us, length us, event | category | flops | bytes accessed | tf_op | source)
XLA Modules:
  0.0 69.1 jit_solution(15277122195698710665)
XLA Ops:
  0.6 0.0 copy-start.5
  0.6 0.0 copy-start.4
  1.3 0.0 copy-done.5
  1.3 0.0 copy-done.4
  1.3 0.0 copy-start
  1.3 1.1 %copy-done = f32[6,4,64,128]{3,2,1,0:T(8,128)S(1)} copy-done((f32[6,4,64,128]{3,2,1,0:T(8,128)S(1)}, f32[6,4,64,128]{3,2,1,0:T(8,128)}, u32[]{:S(2)}) %copy-start) | copy-done | bytes 786456
  2.5 0.0 copy-start.1
  2.5 1.1 %copy-done.1 = bf16[4,3,4,64,128]{4,3,2,1,0:T(8,128)(2,1)S(1)} copy-done((bf16[4,3,4,64,128]{4,3,2,1,0:T(8,128)(2,1)S(1)}, bf16[4,3,4,64,128]{4,3,2,1,0:T(8,128)(2,1)}, u32[]{:S(2)}) %copy-start.1) | copy-done | bytes 786456
  3.6 0.0 copy-start.2
  3.6 0.9 %copy-done.2 = s32[4,64,128]{2,1,0:T(8,128)S(1)} copy-done((s32[4,64,128]{2,1,0:T(8,128)S(1)}, s32[4,64,128]{2,1,0:T(8,128)}, u32[]{:S(2)}) %copy-start.2) | copy-done | bytes 131096
  4.5 0.0 copy-start.3
  4.5 0.8 %copy-done.3 = f32[64,128]{1,0:T(8,128)S(1)} copy-done((f32[64,128]{1,0:T(8,128)S(1)}, f32[64,128]{1,0:T(8,128)}, u32[]{:S(2)}) %copy-start.3) | copy-done | bytes 32792
  5.3 62.2 %shard_map.86 = (f32[6,4,64,128]{3,2,1,0:T(8,128)S(1)}, f32[4,64,128]{2,1,0:T(8,128)S(1)}) custom-call(f32[4]{0:T(128)S(1)} %copy-done.4, s32[1]{0:T(128)S(6)} %copy.11.plane_ref, f32[4]{0:T(128)S(1)} %copy-done.5, f32[6,4,64,128]{3,2,1,0:T(8,128)S(1)} %copy-done, s32[4,64,128]{2,1,0:T(8,128)S(1)} %copy-done.2, f32[64,128]{1,0:T(8,128)S(1)} %copy-done.3, ...), custom_call_target="tpu_custom_call" | custom-call | tf_op jit(solution)/shard_map/pallas_call | solution.py:214
  67.5 0.9 %copy.12 = f32[6,4,64,128]{3,2,1,0:T(8,128)} copy(f32[6,4,64,128]{3,2,1,0:T(8,128)S(1)} %get-tuple-element.4) | data formatting | bytes 1572864
  68.4 0.7 copy.13
Async XLA Ops:
  0.6 0.7 copy-start.5
  0.6 0.7 copy-start.4
  1.3 1.1 %copy-start = (f32[6,4,64,128]{3,2,1,0:T(8,128)S(1)}, f32[6,4,64,128]{3,2,1,0:T(8,128)}, u32[]{:S(2)}) copy-start(f32[6,4,64,128]{3,2,1,0:T(8,128)} %fields_ref.1) | copy-start | bytes 2359300
  2.5 1.1 %copy-start.1 = (bf16[4,3,4,64,128]{4,3,2,1,0:T(8,128)(2,1)S(1)}, bf16[4,3,4,64,128]{4,3,2,1,0:T(8,128)(2,1)}, u32[]{:S(2)}) copy-start(bf16[4,3,4,64,128]{4,3,2,1,0:T(8,128)(2,1)} %forward_ref.1) | copy-start | bytes 2359300
  3.6 0.9 %copy-start.2 = (s32[4,64,128]{2,1,0:T(8,128)S(1)}, s32[4,64,128]{2,1,0:T(8,128)}, u32[]{:S(2)}) copy-start(s32[4,64,128]{2,1,0:T(8,128)} %material_ref.1) | copy-start | bytes 393220
  4.5 0.8 %copy-start.3 = (f32[64,128]{1,0:T(8,128)S(1)}, f32[64,128]{1,0:T(8,128)}, u32[]{:S(2)}) copy-start(f32[64,128]{1,0:T(8,128)} %profile_ref.1) | copy-start | bytes 98308

commit v2 on v0

v2 whole, which is shorter than its diff:
```python
import functools

import jax
import jax.numpy as jnp
from jax import lax
from jax.experimental import pallas as pl
from jax.experimental.pallas import tpu as pltpu
from jax.sharding import PartitionSpec as P

COURANT = 0.5
MESH = pl.DeviceIdType.MESH
AXES = ("gz", "gx", "gy")
STEPS = 4
LOW = 2
HALO = 4
SLOT = 2 * HALO
COPIES = 29


def around(axis, by):
    size = lax.axis_size(axis)
    return lax.rem(lax.axis_index(axis) + by + size, size)


class Copy:
    def __init__(self, k, src, dst, axis, by, send, recv):
        self.end = axis == "gz"
        last = lax.axis_size("gz") - 1
        self.sends = lax.axis_index("gz") != (last if by > 0 else 0)
        self.takes = lax.axis_index("gz") != (0 if by > 0 else last)
        self.copy = pltpu.make_async_remote_copy(
            src_ref=src,
            dst_ref=dst,
            send_sem=send.at[k],
            recv_sem=recv.at[k],
            device_id={axis: around(axis, by)},
            device_id_type=MESH,
        )

    def _on(self, flag, act):
        if self.end:
            pl.when(flag)(act)
        else:
            act()

    def start(self):
        self._on(self.sends, self.copy.start)

    def sent(self):
        self._on(self.sends, self.copy.wait_send)

    def arrived(self):
        self._on(self.takes, self.copy.wait_recv)


def each(planes, act):
    for p in planes:
        act(p)


def run(lo, hi, act):
    if hi - lo == 1:
        act(lo)
    else:
        lax.fori_loop(lo, hi, lambda p, _: (act(p), 0)[1], 0)


def kernel(
    eps_ref,
    plane_ref,
    wave_ref,
    fields,
    material,
    profile,
    forward,
    out_ref,
    grad_ref,
    fa,
    fb,
    ca,
    cb,
    mat,
    prof_a,
    prof_b,
    stored,
    packed,
    y_in,
    border,
    z_border,
    x_in,
    x_mat_in,
    x_prof_in,
    x_border_in,
    x_out,
    x_mat_out,
    said,
    heard,
    local,
    send,
    recv,
):
    _, depth, rows, lanes = fields.shape
    wide = rows + 2 * HALO
    own = pl.ds(0, rows)
    extra = pl.ds(rows, 2 * HALO)
    first, final = pl.ds(0, 8), pl.ds(rows - 8, 8)
    top = LOW + depth
    gz, last = lax.axis_index("gz"), lax.axis_size("gz") - 1
    make = functools.partial(Copy, send=send, recv=recv)

    barrier = pltpu.get_barrier_semaphore()
    for axis in AXES:
        for by in (1, -1):
            pl.semaphore_signal(
                barrier, inc=1, device_id={axis: around(axis, by)}, device_id_type=MESH
            )
    loads = [
        pltpu.make_async_copy(src, dst, local.at[k])
        for k, (src, dst) in enumerate(
            (
                (fields, fa.at[:, pl.ds(LOW, depth), own]),
                (material, mat.at[pl.ds(LOW, depth), own]),
                (profile, prof_a.at[own]),
                (forward, stored),
            )
        )
    ]
    for load in loads:
        load.start()
    pl.semaphore_wait(barrier, 2 * len(AXES))

    planes = [
        make(9, fields.at[pl.ds(0, 2), 0], fa.at[pl.ds(0, 2), top, own], "gz", -1),
        make(0, fields.at[:, depth - 1], fa.at[:, 1, own], "gz", 1),
        make(10, fields.at[pl.ds(2, 4), 0], fa.at[pl.ds(2, 4), top, own], "gz", -1),
        make(2, material.at[pl.ds(depth - 2, 2)], mat.at[pl.ds(0, 2), own], "gz", 1),
        make(12, material.at[0], mat.at[top, own], "gz", -1),
        make(1, fields.at[pl.ds(0, 5), depth - 2], fa.at[pl.ds(0, 5), 0, own], "gz", 1),
        make(11, fields.at[pl.ds(0, 2), 1], fa.at[pl.ds(0, 2), top + 1, own], "gz", -1),
    ]
    tiles = []
    for k, (by, edge) in enumerate(((-1, first), (1, final))):
        tiles += [
            make(19 + 4 * k, fields.at[:, :, edge], x_in.at[k], "gx", by),
            make(20 + 4 * k, material.at[:, edge], x_mat_in.at[k], "gx", by),
            make(21 + 4 * k, profile.at[edge], x_prof_in.at[k], "gx", by),
        ]
    for copy in tiles + planes:
        copy.start()

    lane = lax.broadcasted_iota(jnp.int32, (wide, lanes), 1)
    tile_row = lax.broadcasted_iota(jnp.int32, (8, lanes), 0)
    from_next = tile_row < HALO
    at_first, at_last = lane == 0, lane == lanes - 1

    for load in loads[:3]:
        load.wait()
    per = lanes // SLOT
    sources = [functools.partial(lambda c, p: fa[c, LOW + p, own], c, p) for c in range(6) for p in range(depth)]
    sources += [functools.partial(lambda p: mat[LOW + p, own].astype(jnp.float32), p) for p in range(depth)]
    sources += [lambda: prof_a[own]]
    slot_of = lane[:rows] // SLOT
    for half in range(2):
        filled = jnp.zeros((rows, lanes), jnp.float32)
        for s, read in enumerate(sources[half * per : (half + 1) * per]):
            filled = jnp.where(slot_of == s, pltpu.roll(read(), SLOT * s + HALO, 1), filled)
        packed[half] = filled
    columns = [make(27 + k, packed, y_in.at[k], "gy", by) for k, by in enumerate((-1, 1))]
    for copy in columns:
        copy.start()

    @pl.when(gz == 0)
    def _():
        fa[:, pl.ds(0, LOW)] = jnp.zeros((6, LOW, wide, lanes), jnp.float32)
        mat[pl.ds(0, LOW)] = jnp.zeros((LOW, wide, lanes), jnp.int32)
        z_border[0] = jnp.zeros(z_border.shape[1:], jnp.float32)
        for m in range(2):
            heard[m, 0] = jnp.zeros(heard.shape[2:], jnp.float32)

    @pl.when(gz == last)
    def _():
        fa[:, pl.ds(top, 2)] = jnp.zeros((6, 2, wide, lanes), jnp.float32)
        mat[top] = jnp.zeros((wide, lanes), jnp.int32)
        z_border[1] = jnp.zeros(z_border.shape[1:], jnp.float32)
        for m in range(2):
            heard[m, 1] = jnp.zeros(heard.shape[2:], jnp.float32)

    for copy in tiles:
        copy.arrived()
    for c in range(6):
        for p in range(depth):
            tile = jnp.where(from_next, x_in[0, c, p], x_in[1, c, p])
            x_out[c, p] = tile
            fa[c, LOW + p, extra] = tile
    for p in range(depth):
        tile = jnp.where(from_next, x_mat_in[0, p], x_mat_in[1, p])
        x_mat_out[p] = tile
        mat[LOW + p, extra] = tile
    prof_a[extra] = jnp.where(from_next, x_prof_in[0], x_prof_in[1])
    ghosts = [
        make(3, x_out.at[:, depth - 1], fa.at[:, 1, extra], "gz", 1),
        make(13, x_out.at[:, 0], fa.at[:, top, extra], "gz", -1),
        make(5, x_mat_out.at[pl.ds(depth - 2, 2)], mat.at[pl.ds(0, 2), extra], "gz", 1),
        make(15, x_mat_out.at[0], mat.at[top, extra], "gz", -1),
        make(4, x_out.at[pl.ds(0, 5), depth - 2], fa.at[pl.ds(0, 5), 0, extra], "gz", 1),
        make(14, x_out.at[pl.ds(0, 2), 1], fa.at[pl.ds(0, 2), top + 1, extra], "gz", -1),
    ]
    for copy in ghosts:
        copy.start()

    for copy in columns:
        copy.arrived()
    for half in range(2):
        border[half, own] = jnp.where(
            lane[:rows] % SLOT < HALO, y_in[1, half], y_in[0, half]
        )
    corners = [
        make(22 + 4 * k, border.at[:, edge], x_border_in.at[k], "gx", by)
        for k, (by, edge) in enumerate(((-1, first), (1, final)))
    ]
    for copy in corners:
        copy.start()

    table = [COURANT / jnp.full((1, lanes), eps_ref[m], jnp.float32) for m in range(eps_ref.shape[0])]

    def coef_a(p, keep=None):
        kinds = mat[p]
        value = jnp.broadcast_to(table[0], (wide, lanes))
        for m in range(1, len(table)):
            value = jnp.where(kinds == m, table[m], value)
        ca[p] = value if keep is None else value * keep

    def coef_b(p, kinds, keep=None):
        value = jnp.broadcast_to(table[0], kinds.shape)
        for m in range(1, len(table)):
            value = jnp.where(kinds > m - 0.5, table[m], value)
        cb[p] = value if keep is None else value * keep

    def unpack(ref, s):
        half, s = divmod(s, per)
        return pltpu.roll(ref[half], lanes - (SLOT * s + HALO), 1)

    run(LOW, top, coef_a)
    for copy in corners:
        copy.arrived()
    for half in range(2):
        border[half, extra] = jnp.where(from_next, x_border_in[0, half], x_border_in[1, half])
    borders = [
        make(6, border, z_border.at[0], "gz", 1),
        make(16, border, z_border.at[1], "gz", -1),
    ]
    for copy in borders:
        copy.start()

    for p in range(depth):
        for c in range(6):
            fb[c, LOW + p] = unpack(border, c * depth + p)
        coef_b(LOW + p, unpack(border, 6 * depth + p))
    prof_b[...] = unpack(border, 7 * depth)

    low_rate = COURANT * (gz != 0).astype(jnp.float32)

    def pair(c, p, t=0):
        if t > 0 and c < 2 and isinstance(p, int) and p in (0, top + 1):
            there = heard.at[t - 1, 0 if p == 0 else 1]
            return there[c], pltpu.roll(there[2], lanes // 2, 1) if c else there[2]
        return fa[c, p], fb[c, p]

    def minus(u, v):
        return u[0] - v[0], u[1] - v[1]

    def next_x(u):
        return tuple(pltpu.roll(v, wide - 1, 0) - v for v in u)

    def last_x(u):
        return tuple(v - pltpu.roll(v, 1, 0) for v in u)

    def next_y(u):
        a, b = (pltpu.roll(v, lanes - 1, 1) for v in u)
        return jnp.where(at_last, b, a) - u[0], jnp.where(at_last, a, b) - u[1]

    def last_y(u):
        a, b = (pltpu.roll(v, 1, 1) for v in u)
        return u[0] - jnp.where(at_first, b, a), u[1] - jnp.where(at_first, a, b)

    def put(c, p, value, t):
        fa[c, p], fb[c, p] = value
        if t == STEPS and not (isinstance(p, int) and not LOW <= p < top):
            out_ref[c, p - LOW] = value[0][:rows]

    def magnetic(p, t):
        low = isinstance(p, int) and p < LOW
        rate = low_rate if low else COURANT
        outer = isinstance(p, int) and p == 0

        def push(c, curl):
            old = fa[c, p], fb[c, p]
            put(c, p, tuple(o - rate * k for o, k in zip(old, curl)), t)

        ex, ey, ez = pair(0, p, t - 1), pair(1, p, t - 1), pair(2, p)
        push(3, minus(next_y(ez), minus(pair(1, p + 1, t - 1), ey)))
        push(4, minus(minus(pair(0, p + 1, t - 1), ex), next_x(ez)))
        if not outer:
            push(5, minus(next_x(ey), next_y(ex)))

    def electric(p, t):
        coef = ca[p], cb[p]

        def push(c, curl):
            old = fa[c, p], fb[c, p]
            put(c, p, tuple(o + k * d for o, k, d in zip(old, coef, curl)), t)

        hx, hy = pair(3, p), pair(4, p)
        push(2, minus(last_x(hy), last_y(hx)))
        if isinstance(p, int) and p == 0:
            return
        hz = pair(5, p)
        here = (gz * depth + p - LOW == plane_ref[0]).astype(jnp.float32)
        pushed = wave_ref[t - 1] * here
        curl = minus(last_y(hz), minus(hy, pair(4, p - 1)))
        push(0, (curl[0] + pushed * prof_a[...], curl[1] + pushed * prof_b[...]))
        push(1, minus(minus(hx, pair(3, p - 1)), last_x(hz)))

    def gather(p, t):
        total = jnp.zeros((rows, lanes), jnp.float32) if t == 1 else grad_ref[p - LOW]
        for c in range(3):
            total = total + stored[t - 1, c, p - LOW].astype(jnp.float32) * fa[c, p, own]
        if t == STEPS:
            total = jnp.where(mat[p, own] >= 2, -total, 0.0)
        grad_ref[p - LOW] = total

    def tell(t):
        copies = []
        for k, (p, by) in enumerate(((top - 2, 1), (LOW + 1, -1))):
            words = said.at[t - 1, k]
            words[0], words[1] = fa[0, p], fa[1, p]
            middle = (lane >= lanes // 4) & (lane < 3 * lanes // 4)
            words[2] = jnp.where(middle, pltpu.roll(fb[1, p], lanes // 2, 1), fb[0, p])
            copies.append(make(7 + 10 * k - 1 + t, words, heard.at[t - 1, k], "gz", by))
        for copy in copies:
            copy.start()
        return copies

    a, b = LOW, top - 1
    run(a, b, lambda p: magnetic(p, 1))
    run(a + 1, b, lambda p: electric(p, 1))
    first_told = tell(1)
    loads[3].wait()
    run(a + 1, b, lambda p: gather(p, 1))

    for copy in planes + ghosts + borders:
        copy.arrived()
    coef_a(1)
    for c in range(6):
        fb[c, 1] = unpack(z_border.at[0], c * depth + depth - 1)
    coef_b(1, unpack(z_border.at[0], 6 * depth + depth - 1))
    for c in range(6):
        fb[c, top] = unpack(z_border.at[1], c * depth)
    each((1, b), lambda p: magnetic(p, 1))
    each((a, b), lambda p: electric(p, 1))
    run(a, b, lambda p: magnetic(p, 2))
    each((a, b), lambda p: gather(p, 1))
    run(a + 1, b, lambda p: electric(p, 2))
    second_told = tell(2)
    run(a + 1, b, lambda p: gather(p, 2))

    keep = (gz != last).astype(jnp.float32)
    coef_a(0)
    coef_a(top, keep)
    for c in range(5):
        fb[c, 0] = unpack(z_border.at[0], c * depth + depth - 2)
    coef_b(0, unpack(z_border.at[0], 6 * depth + depth - 2))
    coef_b(top, unpack(z_border.at[1], 6 * depth), keep)
    for c in range(2):
        fb[c, top + 1] = unpack(z_border.at[1], c * depth + 1)
    each((0, top), lambda p: magnetic(p, 1))
    each((0, 1, top), lambda p: electric(p, 1))
    each((1, b), lambda p: magnetic(p, 2))
    each((a, b), lambda p: electric(p, 2))
    each((a, b), lambda p: gather(p, 2))
    run(a, b, lambda p: magnetic(p, 3))
    run(a + 1, b, lambda p: electric(p, 3))
    run(a + 1, b, lambda p: gather(p, 3))
    magnetic(a + 1, 4)

    for copy in first_told:
        copy.arrived()
    each((0, top), lambda p: magnetic(p, 2))
    each((0, 1, top), lambda p: electric(p, 2))
    each((1, b), lambda p: magnetic(p, 3))
    each((a, b), lambda p: electric(p, 3))
    each((a, b), lambda p: gather(p, 3))
    each((a, b - 1), lambda p: magnetic(p, 4))
    each((a + 1, b - 1), lambda p: electric(p, 4))
    each((a + 1, b - 1), lambda p: gather(p, 4))

    for copy in second_told:
        copy.arrived()
    each((0, top), lambda p: magnetic(p, 3))
    each((1, top), lambda p: electric(p, 3))
    each((1, b), lambda p: magnetic(p, 4))
    each((a, b), lambda p: electric(p, 4))
    each((a, b), lambda p: gather(p, 4))

    for copy in planes + tiles + columns + ghosts + corners + borders + first_told + second_told:
        copy.sent()


def on_device(
    fields_in, material, material_eps, source_plane, source_wave, source_profile, forward_fields
):
    depth, rows, lanes = material.shape
    wide = rows + 2 * HALO
    levels = depth + 2 * LOW
    f32 = jnp.float32
    whole = pl.BlockSpec(memory_space=pltpu.VMEM)
    scalars = pl.BlockSpec(memory_space=pltpu.SMEM)
    remote = pl.BlockSpec(memory_space=pltpu.HBM)
    return pl.pallas_call(
        kernel,
        out_shape=(
            jax.ShapeDtypeStruct(fields_in.shape, f32),
            jax.ShapeDtypeStruct(material.shape, f32),
        ),
        in_specs=[scalars] * 3 + [remote] * 4,
        out_specs=(whole, whole),
        scratch_shapes=[
            pltpu.VMEM((6, levels, wide, lanes), f32),
            pltpu.VMEM((6, levels, wide, lanes), f32),
            pltpu.VMEM((levels, wide, lanes), f32),
            pltpu.VMEM((levels, wide, lanes), f32),
            pltpu.VMEM((levels, wide, lanes), jnp.int32),
            pltpu.VMEM((wide, lanes), f32),
            pltpu.VMEM((wide, lanes), f32),
            pltpu.VMEM(forward_fields.shape, forward_fields.dtype),
            pltpu.VMEM((2, rows, lanes), f32),
            pltpu.VMEM((2, 2, rows, lanes), f32),
            pltpu.VMEM((2, wide, lanes), f32),
            pltpu.VMEM((2, 2, wide, lanes), f32),
            pltpu.VMEM((2, 6, depth, 8, lanes), f32),
            pltpu.VMEM((2, depth, 8, lanes), jnp.int32),
            pltpu.VMEM((2, 8, lanes), f32),
            pltpu.VMEM((2, 2, 8, lanes), f32),
            pltpu.VMEM((6, depth, 8, lanes), f32),
            pltpu.VMEM((depth, 8, lanes), jnp.int32),
            pltpu.VMEM((2, 2, 3, wide, lanes), f32),
            pltpu.VMEM((2, 2, 3, wide, lanes), f32),
            pltpu.SemaphoreType.DMA((4,)),
            pltpu.SemaphoreType.DMA((COPIES,)),
            pltpu.SemaphoreType.DMA((COPIES,)),
        ],
        compiler_params=pltpu.CompilerParams(
            collective_id=0, has_side_effects=True, vmem_limit_bytes=40 << 20
        ),
    )(
        material_eps,
        source_plane,
        source_wave,
        fields_in,
        material,
        source_profile,
        forward_fields,
    )


def solution(mesh):
    placed = (
        P(None, "gz", "gx", "gy"),
        P("gz", "gx", "gy"),
        P(),
        P(),
        P(),
        P("gx", "gy"),
        P(None, None, "gz", "gx", "gy"),
    )
    return jax.shard_map(
        on_device,
        mesh=mesh,
        in_specs=placed,
        out_specs=(P(None, "gz", "gx", "gy"), P("gz", "gx", "gy")),
        check_vma=False,
    )
```

time: 193 us -> 66.9 us (0.35)
  the two profiles are of different devices: /device:TPU:9 before, /device:TPU:6 now
where the time goes in v2:
time: 66.9 us; the launch traced here: 66.6 us
  Pallas kernels  59.8 us (89%)
  local copies, waits for them, and re-layouts  5.47 us (8%)
  between operations  1.35 us (2%)
    pallas_call x1, Pallas kernels, on_device(): pl.pallas_call(kernel, out_shape=(jax.ShapeDtypeStruct(fields_in.shape, f...  59.8 us
    unnamed x14, local copies, waits for them, and re-layouts  5.47 us

profile of v2, /device:TPU:6, one launch (start us, length us, event | category | flops | bytes accessed | tf_op | source)
XLA Modules:
  0.0 66.6 jit_solution(3783307232962210387)
XLA Ops:
  0.6 0.0 copy-start.5
  0.6 0.0 copy-start.4
  1.3 0.0 copy-done.5
  1.3 0.0 copy-done.4
  1.3 0.0 copy-start
  1.3 1.1 %copy-done = f32[6,4,64,128]{3,2,1,0:T(8,128)S(1)} copy-done((f32[6,4,64,128]{3,2,1,0:T(8,128)S(1)}, f32[6,4,64,128]{3,2,1,0:T(8,128)}, u32[]{:S(2)}) %copy-start) | copy-done | bytes 786456
  2.5 0.0 copy-start.1
  2.5 1.1 %copy-done.1 = bf16[4,3,4,64,128]{4,3,2,1,0:T(8,128)(2,1)S(1)} copy-done((bf16[4,3,4,64,128]{4,3,2,1,0:T(8,128)(2,1)S(1)}, bf16[4,3,4,64,128]{4,3,2,1,0:T(8,128)(2,1)}, u32[]{:S(2)}) %copy-start.1) | copy-done | bytes 786456
  3.6 0.0 copy-start.2
  3.6 0.9 %copy-done.2 = s32[4,64,128]{2,1,0:T(8,128)S(1)} copy-done((s32[4,64,128]{2,1,0:T(8,128)S(1)}, s32[4,64,128]{2,1,0:T(8,128)}, u32[]{:S(2)}) %copy-start.2) | copy-done | bytes 131096
  4.5 0.0 copy-start.3
  4.5 0.8 %copy-done.3 = f32[64,128]{1,0:T(8,128)S(1)} copy-done((f32[64,128]{1,0:T(8,128)S(1)}, f32[64,128]{1,0:T(8,128)}, u32[]{:S(2)}) %copy-start.3) | copy-done | bytes 32792
  5.3 59.8 %shard_map.86 = (f32[6,4,64,128]{3,2,1,0:T(8,128)S(1)}, f32[4,64,128]{2,1,0:T(8,128)S(1)}) custom-call(f32[4]{0:T(128)S(1)} %copy-done.4, s32[1]{0:T(128)S(6)} %copy.11.plane_ref, f32[4]{0:T(128)S(1)} %copy-done.5, f32[6,4,64,128]{3,2,1,0:T(8,128)S(1)} %copy-done, s32[4,64,128]{2,1,0:T(8,128)S(1)} %copy-done.2, f32[64,128]{1,0:T(8,128)S(1)} %copy-done.3, ...), custom_call_target="tpu_custom_call" | custom-call | tf_op jit(solution)/shard_map/pallas_call | solution.py:419
  65.0 0.9 %copy.12 = f32[6,4,64,128]{3,2,1,0:T(8,128)} copy(f32[6,4,64,128]{3,2,1,0:T(8,128)S(1)} %get-tuple-element.4) | data formatting | bytes 1572864
  65.9 0.7 copy.13
Async XLA Ops:
  0.6 0.7 %copy-start.5 = (f32[4]{0:T(128)S(1)}, f32[4]{0:T(128)}, u32[]{:S(2)}) copy-start(f32[4]{0:T(128)} %wave_ref.1) | copy-start | bytes 52
  0.6 0.7 %copy-start.4 = (f32[4]{0:T(128)S(1)}, f32[4]{0:T(128)}, u32[]{:S(2)}) copy-start(f32[4]{0:T(128)} %eps_ref.1) | copy-start | bytes 52
  1.3 1.1 %copy-start = (f32[6,4,64,128]{3,2,1,0:T(8,128)S(1)}, f32[6,4,64,128]{3,2,1,0:T(8,128)}, u32[]{:S(2)}) copy-start(f32[6,4,64,128]{3,2,1,0:T(8,128)} %fields.1) | copy-start | bytes 2359300
  2.5 1.1 %copy-start.1 = (bf16[4,3,4,64,128]{4,3,2,1,0:T(8,128)(2,1)S(1)}, bf16[4,3,4,64,128]{4,3,2,1,0:T(8,128)(2,1)}, u32[]{:S(2)}) copy-start(bf16[4,3,4,64,128]{4,3,2,1,0:T(8,128)(2,1)} %forward.1) | copy-start | bytes 2359300
  3.6 0.9 %copy-start.2 = (s32[4,64,128]{2,1,0:T(8,128)S(1)}, s32[4,64,128]{2,1,0:T(8,128)}, u32[]{:S(2)}) copy-start(s32[4,64,128]{2,1,0:T(8,128)} %material.1) | copy-start | bytes 393220
  4.5 0.8 %copy-start.3 = (f32[64,128]{1,0:T(8,128)S(1)}, f32[64,128]{1,0:T(8,128)}, u32[]{:S(2)}) copy-start(f32[64,128]{1,0:T(8,128)} %profile.1) | copy-start | bytes 98308

commit v3 on v2

--- a/solution.py
+++ b/solution.py
@@ -9,12 +9,11 @@
 
 COURANT = 0.5
 MESH = pl.DeviceIdType.MESH
-AXES = ("gz", "gx", "gy")
 STEPS = 4
 LOW = 2
 HALO = 4
 SLOT = 2 * HALO
-COPIES = 29
+COPIES = 31
 
 
 def around(axis, by):
@@ -23,8 +22,9 @@
 
 
 class Copy:
-    def __init__(self, k, src, dst, axis, by, send, recv):
-        self.end = axis == "gz"
+    def __init__(self, k, src, dst, send, recv, **steps):
+        self.end = "gz" in steps
+        by = steps.get("gz", 1)
         last = lax.axis_size("gz") - 1
         self.sends = lax.axis_index("gz") != (last if by > 0 else 0)
         self.takes = lax.axis_index("gz") != (0 if by > 0 else last)
@@ -33,7 +33,7 @@
             dst_ref=dst,
             send_sem=send.at[k],
             recv_sem=recv.at[k],
-            device_id={axis: around(axis, by)},
+            device_id={axis: around(axis, n) for axis, n in steps.items()},
             device_id_type=MESH,
         )
 
@@ -87,6 +87,8 @@
     y_in,
     border,
     z_border,
+    x_pack,
+    x_mat_pack,
     x_in,
     x_mat_in,
     x_prof_in,
@@ -109,11 +111,18 @@
     make = functools.partial(Copy, send=send, recv=recv)
 
     barrier = pltpu.get_barrier_semaphore()
-    for axis in AXES:
-        for by in (1, -1):
-            pl.semaphore_signal(
-                barrier, inc=1, device_id={axis: around(axis, by)}, device_id_type=MESH
-            )
+
+    def greet(**steps):
+        there = {axis: around(axis, n) for axis, n in steps.items()}
+        pl.semaphore_signal(barrier, inc=1, device_id=there, device_id_type=MESH)
+
+    pl.when(gz != last)(lambda: greet(gz=1))
+    pl.when(gz != 0)(lambda: greet(gz=-1))
+    for by in (1, -1):
+        greet(gx=by)
+        greet(gy=by)
+        for n in (1, -1):
+            greet(gx=by, gy=n)
     loads = [
         pltpu.make_async_copy(src, dst, local.at[k])
         for k, (src, dst) in enumerate(
@@ -127,25 +136,23 @@
     ]
     for load in loads:
         load.start()
-    pl.semaphore_wait(barrier, 2 * len(AXES))
-
-    planes = [
-        make(9, fields.at[pl.ds(0, 2), 0], fa.at[pl.ds(0, 2), top, own], "gz", -1),
-        make(0, fields.at[:, depth - 1], fa.at[:, 1, own], "gz", 1),
-        make(10, fields.at[pl.ds(2, 4), 0], fa.at[pl.ds(2, 4), top, own], "gz", -1),
-        make(2, material.at[pl.ds(depth - 2, 2)], mat.at[pl.ds(0, 2), own], "gz", 1),
-        make(12, material.at[0], mat.at[top, own], "gz", -1),
-        make(1, fields.at[pl.ds(0, 5), depth - 2], fa.at[pl.ds(0, 5), 0, own], "gz", 1),
-        make(11, fields.at[pl.ds(0, 2), 1], fa.at[pl.ds(0, 2), top + 1, own], "gz", -1),
-    ]
-    tiles = []
-    for k, (by, edge) in enumerate(((-1, first), (1, final))):
-        tiles += [
-            make(19 + 4 * k, fields.at[:, :, edge], x_in.at[k], "gx", by),
-            make(20 + 4 * k, material.at[:, edge], x_mat_in.at[k], "gx", by),
-            make(21 + 4 * k, profile.at[edge], x_prof_in.at[k], "gx", by),
-        ]
-    for copy in tiles + planes:
+    edge = (gz == 0) | (gz == last)
+    pl.semaphore_wait(barrier, jnp.where(edge, 9, 10))
+
+    falling = [
+        make(9, fields.at[:, 0], fa.at[:, top, own], gz=-1),
+        make(12, material.at[0], mat.at[top, own], gz=-1),
+    ]
+    rising = [
+        make(0, fields.at[:, depth - 1], fa.at[:, 1, own], gz=1),
+        make(2, material.at[pl.ds(depth - 2, 2)], mat.at[pl.ds(0, 2), own], gz=1),
+    ]
+    outer = [
+        make(1, fields.at[pl.ds(0, 5), depth - 2], fa.at[pl.ds(0, 5), 0, own], gz=1),
+        make(11, fields.at[pl.ds(0, 2), 1], fa.at[pl.ds(0, 2), top + 1, own], gz=-1),
+    ]
+    planes = falling + rising
+    for copy in falling + rising:
         copy.start()
 
     lane = lax.broadcasted_iota(jnp.int32, (wide, lanes), 1)
@@ -155,18 +162,51 @@
 
     for load in loads[:3]:
         load.wait()
-    per = lanes // SLOT
-    sources = [functools.partial(lambda c, p: fa[c, LOW + p, own], c, p) for c in range(6) for p in range(depth)]
-    sources += [functools.partial(lambda p: mat[LOW + p, own].astype(jnp.float32), p) for p in range(depth)]
-    sources += [lambda: prof_a[own]]
+
+    def turned(tile):
+        return pltpu.roll(tile, HALO, 0)
+
+    tiles = []
+    for k, (by, edge) in enumerate(((-1, first), (1, final))):
+        for h in range(depth // 2):
+            p = LOW + 2 * h
+            for source, dest in [(fa.at[c], x_pack.at[k, c, h]) for c in range(6)] + [
+                (mat, x_mat_pack.at[k, h])
+            ]:
+                one, two = source[p, edge], source[p + 1, edge]
+                one, two = (one, turned(two)) if k == 0 else (turned(one), two)
+                dest[...] = jnp.where(from_next, one, two)
+        tiles += [
+            make(19 + 3 * k, x_pack.at[k], x_in.at[k], gx=by),
+            make(20 + 3 * k, x_mat_pack.at[k], x_mat_in.at[k], gx=by),
+            make(21 + 3 * k, profile.at[edge], x_prof_in.at[k], gx=by),
+        ]
+    for copy in tiles:
+        copy.start()
+
+    def narrow(c, p):
+        return mat[LOW + p, own].astype(jnp.float32) if c == 6 else fa[c, LOW + p, own]
+
+    def place(c, p):
+        return p // 2, 7 * (p % 2) + c
+
+    profile_place = (0, 14)
     slot_of = lane[:rows] // SLOT
     for half in range(2):
         filled = jnp.zeros((rows, lanes), jnp.float32)
-        for s, read in enumerate(sources[half * per : (half + 1) * per]):
-            filled = jnp.where(slot_of == s, pltpu.roll(read(), SLOT * s + HALO, 1), filled)
+        pieces = [(place(c, p)[1], narrow(c, p)) for p in (2 * half, 2 * half + 1) for c in range(7)]
+        if half == profile_place[0]:
+            pieces.append((profile_place[1], prof_a[own]))
+        for s, value in pieces:
+            filled = jnp.where(slot_of == s, pltpu.roll(value, SLOT * s + HALO, 1), filled)
         packed[half] = filled
-    columns = [make(27 + k, packed, y_in.at[k], "gy", by) for k, by in enumerate((-1, 1))]
-    for copy in columns:
+    columns = [make(29 + k, packed, y_in.at[k], gy=by) for k, by in enumerate((-1, 1))]
+    corners = [
+        make(25 + 2 * k + n, packed.at[:, edge], x_border_in.at[k, n], gx=by, gy=way)
+        for k, (by, edge) in enumerate(((-1, first), (1, final)))
+        for n, way in enumerate((-1, 1))
+    ]
+    for copy in corners + columns:
         copy.start()
 
     @pl.when(gz == 0)
@@ -187,40 +227,39 @@
 
     for copy in tiles:
         copy.arrived()
+
+    def meet(after, before, p):
+        after, before = (turned(after), before) if p % 2 else (after, turned(before))
+        return jnp.where(from_next, after, before)
+
     for c in range(6):
         for p in range(depth):
-            tile = jnp.where(from_next, x_in[0, c, p], x_in[1, c, p])
+            tile = meet(x_in[0, c, p // 2], x_in[1, c, p // 2], p)
             x_out[c, p] = tile
             fa[c, LOW + p, extra] = tile
     for p in range(depth):
-        tile = jnp.where(from_next, x_mat_in[0, p], x_mat_in[1, p])
+        tile = meet(x_mat_in[0, p // 2], x_mat_in[1, p // 2], p)
         x_mat_out[p] = tile
         mat[LOW + p, extra] = tile
     prof_a[extra] = jnp.where(from_next, x_prof_in[0], x_prof_in[1])
     ghosts = [
-        make(3, x_out.at[:, depth - 1], fa.at[:, 1, extra], "gz", 1),
-        make(13, x_out.at[:, 0], fa.at[:, top, extra], "gz", -1),
-        make(5, x_mat_out.at[pl.ds(depth - 2, 2)], mat.at[pl.ds(0, 2), extra], "gz", 1),
-        make(15, x_mat_out.at[0], mat.at[top, extra], "gz", -1),
-        make(4, x_out.at[pl.ds(0, 5), depth - 2], fa.at[pl.ds(0, 5), 0, extra], "gz", 1),
-        make(14, x_out.at[pl.ds(0, 2), 1], fa.at[pl.ds(0, 2), top + 1, extra], "gz", -1),
+        make(13, x_out.at[:, 0], fa.at[:, top, extra], gz=-1),
+        make(15, x_mat_out.at[0], mat.at[top, extra], gz=-1),
+        make(3, x_out.at[:, depth - 1], fa.at[:, 1, extra], gz=1),
+        make(5, x_mat_out.at[pl.ds(depth - 2, 2)], mat.at[pl.ds(0, 2), extra], gz=1),
+    ]
+    outer += [
+        make(4, x_out.at[pl.ds(0, 5), depth - 2], fa.at[pl.ds(0, 5), 0, extra], gz=1),
+        make(14, x_out.at[pl.ds(0, 2), 1], fa.at[pl.ds(0, 2), top + 1, extra], gz=-1),
     ]
     for copy in ghosts:
         copy.start()
 
     for copy in columns:
         copy.arrived()
+    from_below = lane % SLOT < HALO
     for half in range(2):
-        border[half, own] = jnp.where(
-            lane[:rows] % SLOT < HALO, y_in[1, half], y_in[0, half]
-        )
-    corners = [
-        make(22 + 4 * k, border.at[:, edge], x_border_in.at[k], "gx", by)
-        for k, (by, edge) in enumerate(((-1, first), (1, final)))
-    ]
-    for copy in corners:
-        copy.start()
-
+        border[half, own] = jnp.where(from_below[:rows], y_in[1, half], y_in[0, half])
     table = [COURANT / jnp.full((1, lanes), eps_ref[m], jnp.float32) for m in range(eps_ref.shape[0])]
 
     def coef_a(p, keep=None):
@@ -236,27 +275,27 @@
             value = jnp.where(kinds > m - 0.5, table[m], value)
         cb[p] = value if keep is None else value * keep
 
-    def unpack(ref, s):
-        half, s = divmod(s, per)
-        return pltpu.roll(ref[half], lanes - (SLOT * s + HALO), 1)
+    def unpack(value, s):
+        return pltpu.roll(value, lanes - (SLOT * s + HALO), 1)
 
     run(LOW, top, coef_a)
     for copy in corners:
         copy.arrived()
     for half in range(2):
-        border[half, extra] = jnp.where(from_next, x_border_in[0, half], x_border_in[1, half])
+        tile = jnp.where(from_next, x_border_in[0, :, half], x_border_in[1, :, half])
+        border[half, extra] = jnp.where(from_below[:8], tile[1], tile[0])
     borders = [
-        make(6, border, z_border.at[0], "gz", 1),
-        make(16, border, z_border.at[1], "gz", -1),
-    ]
-    for copy in borders:
+        make(6, border.at[1], z_border.at[0], gz=1),
+        make(16, border.at[0], z_border.at[1], gz=-1),
+    ]
+    for copy in borders + outer:
         copy.start()
 
     for p in range(depth):
         for c in range(6):
-            fb[c, LOW + p] = unpack(border, c * depth + p)
-        coef_b(LOW + p, unpack(border, 6 * depth + p))
-    prof_b[...] = unpack(border, 7 * depth)
+            fb[c, LOW + p] = unpack(border[place(c, p)[0]], place(c, p)[1])
+        coef_b(LOW + p, unpack(border[place(6, p)[0]], place(6, p)[1]))
+    prof_b[...] = unpack(border[profile_place[0]], profile_place[1])
 
     low_rate = COURANT * (gz != 0).astype(jnp.float32)
 
@@ -336,7 +375,7 @@
             words[0], words[1] = fa[0, p], fa[1, p]
             middle = (lane >= lanes // 4) & (lane < 3 * lanes // 4)
             words[2] = jnp.where(middle, pltpu.roll(fb[1, p], lanes // 2, 1), fb[0, p])
-            copies.append(make(7 + 10 * k - 1 + t, words, heard.at[t - 1, k], "gz", by))
+            copies.append(make(7 + 10 * k - 1 + t, words, heard.at[t - 1, k], gz=by))
         for copy in copies:
             copy.start()
         return copies
@@ -352,10 +391,10 @@
         copy.arrived()
     coef_a(1)
     for c in range(6):
-        fb[c, 1] = unpack(z_border.at[0], c * depth + depth - 1)
-    coef_b(1, unpack(z_border.at[0], 6 * depth + depth - 1))
+        fb[c, 1] = unpack(z_border[0], place(c, depth - 1)[1])
+    coef_b(1, unpack(z_border[0], place(6, depth - 1)[1]))
     for c in range(6):
-        fb[c, top] = unpack(z_border.at[1], c * depth)
+        fb[c, top] = unpack(z_border[1], place(c, 0)[1])
     each((1, b), lambda p: magnetic(p, 1))
     each((a, b), lambda p: electric(p, 1))
     run(a, b, lambda p: magnetic(p, 2))
@@ -364,15 +403,17 @@
     second_told = tell(2)
     run(a + 1, b, lambda p: gather(p, 2))
 
+    for copy in outer:
+        copy.arrived()
     keep = (gz != last).astype(jnp.float32)
     coef_a(0)
     coef_a(top, keep)
     for c in range(5):
-        fb[c, 0] = unpack(z_border.at[0], c * depth + depth - 2)
-    coef_b(0, unpack(z_border.at[0], 6 * depth + depth - 2))
-    coef_b(top, unpack(z_border.at[1], 6 * depth), keep)
+        fb[c, 0] = unpack(z_border[0], place(c, depth - 2)[1])
+    coef_b(0, unpack(z_border[0], place(6, depth - 2)[1]))
+    coef_b(top, unpack(z_border[1], place(6, 0)[1]), keep)
     for c in range(2):
-        fb[c, top + 1] = unpack(z_border.at[1], c * depth + 1)
+        fb[c, top + 1] = unpack(z_border[1], place(c, 1)[1])
     each((0, top), lambda p: magnetic(p, 1))
     each((0, 1, top), lambda p: electric(p, 1))
     each((1, b), lambda p: magnetic(p, 2))
@@ -402,7 +443,7 @@
     each((a, b), lambda p: electric(p, 4))
     each((a, b), lambda p: gather(p, 4))
 
-    for copy in planes + tiles + columns + ghosts + corners + borders + first_told + second_told:
+    for copy in planes + outer + tiles + columns + ghosts + corners + borders + first_told + second_told:
         copy.sent()
 
 
@@ -436,11 +477,13 @@
             pltpu.VMEM((2, rows, lanes), f32),
             pltpu.VMEM((2, 2, rows, lanes), f32),
             pltpu.VMEM((2, wide, lanes), f32),
-            pltpu.VMEM((2, 2, wide, lanes), f32),
-            pltpu.VMEM((2, 6, depth, 8, lanes), f32),
-            pltpu.VMEM((2, depth, 8, lanes), jnp.int32),
+            pltpu.VMEM((2, wide, lanes), f32),
+            pltpu.VMEM((2, 6, depth // 2, 8, lanes), f32),
+            pltpu.VMEM((2, depth // 2, 8, lanes), jnp.int32),
+            pltpu.VMEM((2, 6, depth // 2, 8, lanes), f32),
+            pltpu.VMEM((2, depth // 2, 8, lanes), jnp.int32),
             pltpu.VMEM((2, 8, lanes), f32),
-            pltpu.VMEM((2, 2, 8, lanes), f32),
+            pltpu.VMEM((2, 2, 2, 8, lanes), f32),
             pltpu.VMEM((6, depth, 8, lanes), f32),
             pltpu.VMEM((depth, 8, lanes), jnp.int32),
             pltpu.VMEM((2, 2, 3, wide, lanes), f32),
@@ -450,7 +493,7 @@
             pltpu.SemaphoreType.DMA((COPIES,)),
         ],
         compiler_params=pltpu.CompilerParams(
-            collective_id=0, has_side_effects=True, vmem_limit_bytes=40 << 20
+            collective_id=0, has_side_effects=True, vmem_limit_bytes=60 << 20
         ),
     )(
         material_eps,

time: 66.9 us -> 56.6 us (0.85)
  the two profiles are of different devices: /device:TPU:6 before, /device:TPU:16 now
where the time goes in v3:
time: 56.6 us; the launch traced here: 56.4 us
  Pallas kernels  52.3 us (92%)
  local copies, waits for them, and re-layouts  2.78 us (5%)
  between operations  1.29 us (2%)
    pallas_call x1, Pallas kernels, on_device(): pl.pallas_call(kernel, out_shape=(jax.ShapeDtypeStruct(fields_in.shape, f...  52.3 us
    unnamed x4, local copies, waits for them, and re-layouts  2.78 us

profile of v3, /device:TPU:16, one launch (start us, length us, event | category | flops | bytes accessed | tf_op | source)
XLA Modules:
  0.0 56.4 jit_solution(4302854797037719157)
XLA Ops:
  1.3 52.3 %shard_map.86 = (f32[6,4,64,128]{3,2,1,0:T(8,128)}, f32[4,64,128]{2,1,0:T(8,128)}) custom-call(f32[4]{0:T(128)} %eps_ref.1, s32[1]{0:T(128)S(6)} %copy.11.plane_ref, f32[4]{0:T(128)} %wave_ref.1, f32[6,4,64,128]{3,2,1,0:T(8,128)} %fields.1, s32[4,64,128]{2,1,0:T(8,128)} %material.1, f32[64,128]{1,0:T(8,128)} %profile.1, bf16[4,3,4,64,128]{4,3,2,1,0:T(8,128)(2,1)} %forward.1), custom_call_target="tpu_custom_call" | custom-call | tf_op jit(solution)/shard_map/pallas_call | solution.py:460
  53.6 0.0 copy-start
  53.6 2.1 %copy.12 = f32[6,4,64,128]{3,2,1,0:T(8,128)} copy(f32[6,4,64,128]{3,2,1,0:T(8,128)} %get-tuple-element.4) | data formatting | bytes 1572864
  55.7 0.0 copy-done
  55.7 0.7 %copy.13 = f32[4,64,128]{2,1,0:T(8,128)} copy(f32[4,64,128]{2,1,0:T(8,128)S(1)} %copy-done) | data formatting | bytes 262144
Async XLA Ops:
  53.6 2.1 %copy-start = (f32[4,64,128]{2,1,0:T(8,128)S(1)}, f32[4,64,128]{2,1,0:T(8,128)}, u32[]{:S(2)}) copy-start(f32[4,64,128]{2,1,0:T(8,128)} %get-tuple-element.5) | copy-start | bytes 393220

commit v4 on v3

--- a/solution.py
+++ b/solution.py
@@ -14,6 +14,7 @@
 HALO = 4
 SLOT = 2 * HALO
 COPIES = 31
+CHIPS_Z = 16
 
 
 def around(axis, by):
@@ -152,8 +153,14 @@
         make(11, fields.at[pl.ds(0, 2), 1], fa.at[pl.ds(0, 2), top + 1, own], gz=-1),
     ]
     planes = falling + rising
-    for copy in falling + rising:
+    turn = gz % CHIPS_Z == 0
+    for copy in rising:
         copy.start()
+
+    @pl.when(~turn)
+    def _():
+        for copy in falling:
+            copy.start()
 
     lane = lax.broadcasted_iota(jnp.int32, (wide, lanes), 1)
     tile_row = lax.broadcasted_iota(jnp.int32, (8, lanes), 0)
@@ -227,6 +234,11 @@
 
     for copy in tiles:
         copy.arrived()
+
+    @pl.when(turn)
+    def _():
+        for copy in falling:
+            copy.start()
 
     def meet(after, before, p):
         after, before = (turned(after), before) if p % 2 else (after, turned(before))

time: 56.6 us -> 49 us (0.87)
  the two profiles are of different devices: /device:TPU:16 before, /device:TPU:9 now
where the time goes in v4:
time: 49 us; the launch traced here: 48.8 us
  Pallas kernels  44.7 us (91%)
  local copies, waits for them, and re-layouts  2.78 us (6%)
  between operations  1.29 us (3%)
    pallas_call x1, Pallas kernels, on_device(): pl.pallas_call(kernel, out_shape=(jax.ShapeDtypeStruct(fields_in.shape, f...  44.7 us
    unnamed x4, local copies, waits for them, and re-layouts  2.78 us

profile of v4, /device:TPU:9, one launch (start us, length us, event | category | flops | bytes accessed | tf_op | source)
XLA Modules:
  0.0 48.8 jit_solution(4383553210556061030)
XLA Ops:
  1.3 44.7 %shard_map.86 = (f32[6,4,64,128]{3,2,1,0:T(8,128)}, f32[4,64,128]{2,1,0:T(8,128)}) custom-call(f32[4]{0:T(128)} %eps_ref.1, s32[1]{0:T(128)S(6)} %copy.11.plane_ref, f32[4]{0:T(128)} %wave_ref.1, f32[6,4,64,128]{3,2,1,0:T(8,128)} %fields.1, s32[4,64,128]{2,1,0:T(8,128)} %material.1, f32[64,128]{1,0:T(8,128)} %profile.1, bf16[4,3,4,64,128]{4,3,2,1,0:T(8,128)(2,1)} %forward.1), custom_call_target="tpu_custom_call" | custom-call | tf_op jit(solution)/shard_map/pallas_call | solution.py:472
  46.0 0.0 copy-start
  46.0 2.1 %copy.12 = f32[6,4,64,128]{3,2,1,0:T(8,128)} copy(f32[6,4,64,128]{3,2,1,0:T(8,128)} %get-tuple-element.4) | data formatting | bytes 1572864
  48.2 0.0 copy-done
  48.2 0.7 %copy.13 = f32[4,64,128]{2,1,0:T(8,128)} copy(f32[4,64,128]{2,1,0:T(8,128)S(1)} %copy-done) | data formatting | bytes 262144
Async XLA Ops:
  46.0 2.1 %copy-start = (f32[4,64,128]{2,1,0:T(8,128)S(1)}, f32[4,64,128]{2,1,0:T(8,128)}, u32[]{:S(2)}) copy-start(f32[4,64,128]{2,1,0:T(8,128)} %get-tuple-element.5) | copy-start | bytes 393220

commit v5 on v4

--- a/solution.py
+++ b/solution.py
@@ -74,6 +74,8 @@
     material,
     profile,
     forward,
+    out,
+    grad,
     out_ref,
     grad_ref,
     fa,
@@ -98,6 +100,7 @@
     x_mat_out,
     said,
     heard,
+    heard_b,
     local,
     send,
     recv,
@@ -135,7 +138,7 @@
             )
         )
     ]
-    for load in loads:
+    for load in loads[:3]:
         load.start()
     edge = (gz == 0) | (gz == last)
     pl.semaphore_wait(barrier, jnp.where(edge, 9, 10))
@@ -215,6 +218,7 @@
     ]
     for copy in corners + columns:
         copy.start()
+    loads[3].start()
 
     @pl.when(gz == 0)
     def _():
@@ -313,8 +317,8 @@
 
     def pair(c, p, t=0):
         if t > 0 and c < 2 and isinstance(p, int) and p in (0, top + 1):
-            there = heard.at[t - 1, 0 if p == 0 else 1]
-            return there[c], pltpu.roll(there[2], lanes // 2, 1) if c else there[2]
+            side = 0 if p == 0 else 1
+            return heard[t - 1, side, pl.ds(c * wide, wide)], heard_b[t - 1, side, c]
         return fa[c, p], fb[c, p]
 
     def minus(u, v):
@@ -335,14 +339,16 @@
         return u[0] - jnp.where(at_first, b, a), u[1] - jnp.where(at_first, a, b)
 
     def put(c, p, value, t):
-        fa[c, p], fb[c, p] = value
+        fa[c, p] = value[0]
+        if t < STEPS or c > 2:
+            fb[c, p] = value[1]
         if t == STEPS and not (isinstance(p, int) and not LOW <= p < top):
             out_ref[c, p - LOW] = value[0][:rows]
 
     def magnetic(p, t):
         low = isinstance(p, int) and p < LOW
         rate = low_rate if low else COURANT
-        outer = isinstance(p, int) and p == 0
+        outer = isinstance(p, int) and (p == 0 or p < LOW and t == STEPS)
 
         def push(c, curl):
             old = fa[c, p], fb[c, p]
@@ -362,7 +368,8 @@
             put(c, p, tuple(o + k * d for o, k, d in zip(old, coef, curl)), t)
 
         hx, hy = pair(3, p), pair(4, p)
-        push(2, minus(last_x(hy), last_y(hx)))
+        if not (isinstance(p, int) and p == top and t == STEPS - 1):
+            push(2, minus(last_x(hy), last_y(hx)))
         if isinstance(p, int) and p == 0:
             return
         hz = pair(5, p)
@@ -380,13 +387,34 @@
             total = jnp.where(mat[p, own] >= 2, -total, 0.0)
         grad_ref[p - LOW] = total
 
+    folds = lanes // (2 * SLOT)
+    fold = ((lane[:8] + HALO) % lanes) // (2 * SLOT)
+
+    def unfold(t):
+        for side in range(2):
+            for i in range(folds + 1):
+                part = heard[t - 1, side, pl.ds(2 * wide + 8 * (i // folds), 8)]
+                for c in range(2):
+                    by = (2 * SLOT * (i % folds) + SLOT * c) % lanes
+                    heard_b[t - 1, side, c, pl.ds(8 * i, 8)] = (
+                        pltpu.roll(part, lanes - by, 1) if by else part
+                    )
+
     def tell(t):
         copies = []
         for k, (p, by) in enumerate(((top - 2, 1), (LOW + 1, -1))):
             words = said.at[t - 1, k]
-            words[0], words[1] = fa[0, p], fa[1, p]
-            middle = (lane >= lanes // 4) & (lane < 3 * lanes // 4)
-            words[2] = jnp.where(middle, pltpu.roll(fb[1, p], lanes // 2, 1), fb[0, p])
+            words[pl.ds(0, wide)], words[pl.ds(wide, wide)] = fa[0, p], fa[1, p]
+            ghost = jnp.where(
+                (lane >= HALO) & (lane < HALO + SLOT), pltpu.roll(fb[1, p], SLOT, 1), fb[0, p]
+            )
+            filled = ghost[:8]
+            for i in range(1, folds):
+                turn_by = 2 * SLOT * i
+                part = pltpu.roll(ghost[8 * i : 8 * i + 8], turn_by, 1)
+                filled = jnp.where(fold == i, part, filled)
+            words[pl.ds(2 * wide, 8)] = filled
+            words[pl.ds(2 * wide + 8, 8)] = ghost[8 * folds :]
             copies.append(make(7 + 10 * k - 1 + t, words, heard.at[t - 1, k], gz=by))
         for copy in copies:
             copy.start()
@@ -410,9 +438,9 @@
     each((1, b), lambda p: magnetic(p, 1))
     each((a, b), lambda p: electric(p, 1))
     run(a, b, lambda p: magnetic(p, 2))
-    each((a, b), lambda p: gather(p, 1))
     run(a + 1, b, lambda p: electric(p, 2))
     second_told = tell(2)
+    each((a, b), lambda p: gather(p, 1))
     run(a + 1, b, lambda p: gather(p, 2))
 
     for copy in outer:
@@ -438,6 +466,7 @@
 
     for copy in first_told:
         copy.arrived()
+    unfold(1)
     each((0, top), lambda p: magnetic(p, 2))
     each((0, 1, top), lambda p: electric(p, 2))
     each((1, b), lambda p: magnetic(p, 3))
@@ -447,16 +476,46 @@
     each((a + 1, b - 1), lambda p: electric(p, 4))
     each((a + 1, b - 1), lambda p: gather(p, 4))
 
+    stores = []
+
+    def store(planes_at):
+        for k, (src, dst) in enumerate(((out_ref, out), (grad_ref, grad))):
+            there = (slice(None), planes_at) if k == 0 else (planes_at,)
+            stores.append(
+                pltpu.make_async_copy(src.at[there], dst.at[there], local.at[4 + len(stores)])
+            )
+            stores[-1].start()
+
+    store(pl.ds(1, depth - 2))
     for copy in second_told:
         copy.arrived()
+    unfold(2)
     each((0, top), lambda p: magnetic(p, 3))
     each((1, top), lambda p: electric(p, 3))
     each((1, b), lambda p: magnetic(p, 4))
     each((a, b), lambda p: electric(p, 4))
     each((a, b), lambda p: gather(p, 4))
 
+    store(pl.ds(0, 1))
+    store(pl.ds(depth - 1, 1))
+    for copy in stores:
+        copy.wait()
     for copy in planes + outer + tiles + columns + ghosts + corners + borders + first_told + second_told:
         copy.sent()
+
+
+def hand_on(fields, grad, fields_out, grad_out, staged, staged_grad, sem):
+    parts = [(fields.at[c], staged.at[c], fields_out.at[c]) for c in range(6)]
+    parts.append((grad, staged_grad, grad_out))
+    inward = [pltpu.make_async_copy(a, b, sem.at[k]) for k, (a, b, _) in enumerate(parts)]
+    outward = [pltpu.make_async_copy(b, c, sem.at[7 + k]) for k, (_, b, c) in enumerate(parts)]
+    for copy in inward:
+        copy.start()
+    for one, two in zip(inward, outward):
+        one.wait()
+        two.start()
+    for copy in outward:
+        copy.wait()
 
 
 def on_device(
@@ -466,18 +525,19 @@
     wide = rows + 2 * HALO
     levels = depth + 2 * LOW
     f32 = jnp.float32
-    whole = pl.BlockSpec(memory_space=pltpu.VMEM)
     scalars = pl.BlockSpec(memory_space=pltpu.SMEM)
     remote = pl.BlockSpec(memory_space=pltpu.HBM)
-    return pl.pallas_call(
+    fields_out, eps_grad = pl.pallas_call(
         kernel,
         out_shape=(
             jax.ShapeDtypeStruct(fields_in.shape, f32),
             jax.ShapeDtypeStruct(material.shape, f32),
         ),
         in_specs=[scalars] * 3 + [remote] * 4,
-        out_specs=(whole, whole),
+        out_specs=(remote, remote),
         scratch_shapes=[
+            pltpu.VMEM(fields_in.shape, f32),
+            pltpu.VMEM(material.shape, f32),
             pltpu.VMEM((6, levels, wide, lanes), f32),
             pltpu.VMEM((6, levels, wide, lanes), f32),
             pltpu.VMEM((levels, wide, lanes), f32),
@@ -498,9 +558,10 @@
             pltpu.VMEM((2, 2, 2, 8, lanes), f32),
             pltpu.VMEM((6, depth, 8, lanes), f32),
             pltpu.VMEM((depth, 8, lanes), jnp.int32),
-            pltpu.VMEM((2, 2, 3, wide, lanes), f32),
-            pltpu.VMEM((2, 2, 3, wide, lanes), f32),
-            pltpu.SemaphoreType.DMA((4,)),
+            pltpu.VMEM((2, 2, 2 * wide + 16, lanes), f32),
+            pltpu.VMEM((2, 2, 2 * wide + 16, lanes), f32),
+            pltpu.VMEM((2, 2, 2, wide, lanes), f32),
+            pltpu.SemaphoreType.DMA((10,)),
             pltpu.SemaphoreType.DMA((COPIES,)),
             pltpu.SemaphoreType.DMA((COPIES,)),
         ],
@@ -516,6 +577,21 @@
         source_profile,
         forward_fields,
     )
+    return pl.pallas_call(
+        hand_on,
+        out_shape=(
+            jax.ShapeDtypeStruct(fields_in.shape, f32),
+            jax.ShapeDtypeStruct(material.shape, f32),
+        ),
+        in_specs=[remote] * 2,
+        out_specs=(remote, remote),
+        scratch_shapes=[
+            pltpu.VMEM(fields_in.shape, f32),
+            pltpu.VMEM(material.shape, f32),
+            pltpu.SemaphoreType.DMA((14,)),
+        ],
+        compiler_params=pltpu.CompilerParams(vmem_limit_bytes=60 << 20),
+    )(fields_out, eps_grad)
 
 
 def solution(mesh):

time: 49 us -> 47.4 us (0.967)
  local copies, waits for them, and re-layouts: 2.78 us -> 0 us
  Pallas kernels: 44.7 us -> 45.9 us
    unnamed x4 -> x0, local copies, waits for them, and re-layouts: 2.78 us -> none
    pallas_call x0 -> x1, Pallas kernels: none -> 2.03 us  [on_device(): pl.pallas_call(hand_on, out_shape=(jax.ShapeDtypeStruct(fields_in.shape,...]
    pallas_call x1, Pallas kernels: 44.7 us -> 43.9 us  [on_device(): pl.pallas_call(kernel, out_shape=(jax.ShapeDtypeStruct(fields_in.shape, f...]
where the time goes in v5:
time: 47.4 us; the launch traced here: 47.2 us
  Pallas kernels  45.9 us (97%)
  between operations  1.29 us (3%)
    pallas_call x1, Pallas kernels, on_device(): pl.pallas_call(kernel, out_shape=(jax.ShapeDtypeStruct(fields_in.shape, f...  43.9 us
    pallas_call x1, Pallas kernels, on_device(): pl.pallas_call(hand_on, out_shape=(jax.ShapeDtypeStruct(fields_in.shape,...  2.03 us

profile of v5, /device:TPU:9, one launch (start us, length us, event | category | flops | bytes accessed | tf_op | source)
XLA Modules:
  0.0 47.2 jit_solution(17716997826112679598)
XLA Ops:
  1.3 43.9 %shard_map.86 = (f32[6,4,64,128]{3,2,1,0:T(8,128)}, f32[4,64,128]{2,1,0:T(8,128)}) custom-call(f32[4]{0:T(128)} %eps_ref.1, s32[1]{0:T(128)S(6)} %copy.9.plane_ref, f32[4]{0:T(128)} %wave_ref.1, f32[6,4,64,128]{3,2,1,0:T(8,128)} %fields.1, s32[4,64,128]{2,1,0:T(8,128)} %material.1, f32[64,128]{1,0:T(8,128)} %profile.1, bf16[4,3,4,64,128]{4,3,2,1,0:T(8,128)(2,1)} %forward.1), custom_call_target="tpu_custom_call" | custom-call | tf_op jit(solution)/shard_map/pallas_call | solution.py:530
  45.2 2.0 %shard_map.87 = (f32[6,4,64,128]{3,2,1,0:T(8,128)}, f32[4,64,128]{2,1,0:T(8,128)}) custom-call(f32[6,4,64,128]{3,2,1,0:T(8,128)} %get-tuple-element.4.fields, f32[4,64,128]{2,1,0:T(8,128)} %get-tuple-element.5.grad), custom_call_target="tpu_custom_call" | custom-call | tf_op jit(solution)/shard_map/pallas_call | solution.py:580

commit v6 on v5

--- a/solution.py
+++ b/solution.py
@@ -92,6 +92,7 @@
     z_border,
     x_pack,
     x_mat_pack,
+    near,
     x_in,
     x_mat_in,
     x_prof_in,
@@ -138,7 +139,11 @@
             )
         )
     ]
-    for load in loads[:3]:
+    edges = [
+        pltpu.make_async_copy(fields.at[:, :, edge], near.at[k], local.at[10 + k])
+        for k, edge in enumerate((first, final))
+    ]
+    for load in edges + [loads[1], loads[0], loads[2]]:
         load.start()
     edge = (gz == 0) | (gz == last)
     pl.semaphore_wait(barrier, jnp.where(edge, 9, 10))
@@ -170,7 +175,7 @@
     from_next = tile_row < HALO
     at_first, at_last = lane == 0, lane == lanes - 1
 
-    for load in loads[:3]:
+    for load in edges + [loads[1]]:
         load.wait()
 
     def turned(tile):
@@ -180,10 +185,8 @@
     for k, (by, edge) in enumerate(((-1, first), (1, final))):
         for h in range(depth // 2):
             p = LOW + 2 * h
-            for source, dest in [(fa.at[c], x_pack.at[k, c, h]) for c in range(6)] + [
-                (mat, x_mat_pack.at[k, h])
-            ]:
-                one, two = source[p, edge], source[p + 1, edge]
+            pairs = [(near[k, c, 2 * h], near[k, c, 2 * h + 1], x_pack.at[k, c, h]) for c in range(6)]
+            for one, two, dest in pairs + [(mat[p, edge], mat[p + 1, edge], x_mat_pack.at[k, h])]:
                 one, two = (one, turned(two)) if k == 0 else (turned(one), two)
                 dest[...] = jnp.where(from_next, one, two)
         tiles += [
@@ -193,6 +196,8 @@
         ]
     for copy in tiles:
         copy.start()
+    loads[0].wait()
+    loads[2].wait()
 
     def narrow(c, p):
         return mat[LOW + p, own].astype(jnp.float32) if c == 6 else fa[c, LOW + p, own]
@@ -390,8 +395,8 @@
     folds = lanes // (2 * SLOT)
     fold = ((lane[:8] + HALO) % lanes) // (2 * SLOT)
 
-    def unfold(t):
-        for side in range(2):
+    def unfold(t, sides=(0, 1)):
+        for side in sides:
             for i in range(folds + 1):
                 part = heard[t - 1, side, pl.ds(2 * wide + 8 * (i // folds), 8)]
                 for c in range(2):
@@ -400,9 +405,10 @@
                         pltpu.roll(part, lanes - by, 1) if by else part
                     )
 
-    def tell(t):
+    def tell(t, sides=(0, 1)):
         copies = []
-        for k, (p, by) in enumerate(((top - 2, 1), (LOW + 1, -1))):
+        for k in sides:
+            p, by = ((top - 2, 1), (LOW + 1, -1))[k]
             words = said.at[t - 1, k]
             words[pl.ds(0, wide)], words[pl.ds(wide, wide)] = fa[0, p], fa[1, p]
             ghost = jnp.where(
@@ -427,19 +433,29 @@
     loads[3].wait()
     run(a + 1, b, lambda p: gather(p, 1))
 
-    for copy in planes + ghosts + borders:
+    magnetic(a + 1, 2)
+
+    for copy in falling + ghosts[:2] + borders[1:]:
+        copy.arrived()
+    for c in range(6):
+        fb[c, top] = unpack(z_border[1], place(c, 0)[1])
+    magnetic(b, 1)
+    electric(b, 1)
+    magnetic(b - 1, 2)
+    electric(b - 1, 2)
+    told_up = tell(2, (0,))
+
+    for copy in rising + ghosts[2:] + borders[:1]:
         copy.arrived()
     coef_a(1)
     for c in range(6):
         fb[c, 1] = unpack(z_border[0], place(c, depth - 1)[1])
     coef_b(1, unpack(z_border[0], place(6, depth - 1)[1]))
-    for c in range(6):
-        fb[c, top] = unpack(z_border[1], place(c, 0)[1])
-    each((1, b), lambda p: magnetic(p, 1))
-    each((a, b), lambda p: electric(p, 1))
-    run(a, b, lambda p: magnetic(p, 2))
-    run(a + 1, b, lambda p: electric(p, 2))
-    second_told = tell(2)
+    magnetic(1, 1)
+    electric(a, 1)
+    magnetic(a, 2)
+    electric(a + 1, 2)
+    told_down = tell(2, (1,))
     each((a, b), lambda p: gather(p, 1))
     run(a + 1, b, lambda p: gather(p, 2))
 
@@ -487,28 +503,31 @@
             stores[-1].start()
 
     store(pl.ds(1, depth - 2))
-    for copy in second_told:
-        copy.arrived()
-    unfold(2)
-    each((0, top), lambda p: magnetic(p, 3))
-    each((1, top), lambda p: electric(p, 3))
-    each((1, b), lambda p: magnetic(p, 4))
-    each((a, b), lambda p: electric(p, 4))
-    each((a, b), lambda p: gather(p, 4))
-
-    store(pl.ds(0, 1))
-    store(pl.ds(depth - 1, 1))
+    for side, copies, outermost, block in ((1, told_down, top, b), (0, told_up, 0, a)):
+        for copy in copies:
+            copy.arrived()
+        unfold(2, (side,))
+        magnetic(outermost, 3)
+        electric(top if side else 1, 3)
+        magnetic(b if side else 1, 4)
+        electric(block, 4)
+        gather(block, 4)
+        store(pl.ds(block - LOW, 1))
     for copy in stores:
         copy.wait()
-    for copy in planes + outer + tiles + columns + ghosts + corners + borders + first_told + second_told:
+    for copy in planes + outer + tiles + columns + ghosts + corners + borders + first_told + told_up + told_down:
         copy.sent()
 
 
 def hand_on(fields, grad, fields_out, grad_out, staged, staged_grad, sem):
-    parts = [(fields.at[c], staged.at[c], fields_out.at[c]) for c in range(6)]
-    parts.append((grad, staged_grad, grad_out))
+    depth = grad.shape[0]
+    parts = [(grad, staged_grad, grad_out)]
+    for c in range(6):
+        for p in range(0, depth, 2):
+            at = (c, pl.ds(p, 2))
+            parts.append((fields.at[at], staged.at[at], fields_out.at[at]))
     inward = [pltpu.make_async_copy(a, b, sem.at[k]) for k, (a, b, _) in enumerate(parts)]
-    outward = [pltpu.make_async_copy(b, c, sem.at[7 + k]) for k, (_, b, c) in enumerate(parts)]
+    outward = [pltpu.make_async_copy(b, c, sem.at[len(parts) + k]) for k, (_, b, c) in enumerate(parts)]
     for copy in inward:
         copy.start()
     for one, two in zip(inward, outward):
@@ -552,6 +571,7 @@
             pltpu.VMEM((2, wide, lanes), f32),
             pltpu.VMEM((2, 6, depth // 2, 8, lanes), f32),
             pltpu.VMEM((2, depth // 2, 8, lanes), jnp.int32),
+            pltpu.VMEM((2, 6, depth, 8, lanes), f32),
             pltpu.VMEM((2, 6, depth // 2, 8, lanes), f32),
             pltpu.VMEM((2, depth // 2, 8, lanes), jnp.int32),
             pltpu.VMEM((2, 8, lanes), f32),
@@ -561,7 +581,7 @@
             pltpu.VMEM((2, 2, 2 * wide + 16, lanes), f32),
             pltpu.VMEM((2, 2, 2 * wide + 16, lanes), f32),
             pltpu.VMEM((2, 2, 2, wide, lanes), f32),
-            pltpu.SemaphoreType.DMA((10,)),
+            pltpu.SemaphoreType.DMA((12,)),
             pltpu.SemaphoreType.DMA((COPIES,)),
             pltpu.SemaphoreType.DMA((COPIES,)),
         ],
@@ -588,7 +608,7 @@
         scratch_shapes=[
             pltpu.VMEM(fields_in.shape, f32),
             pltpu.VMEM(material.shape, f32),
-            pltpu.SemaphoreType.DMA((14,)),
+            pltpu.SemaphoreType.DMA((26,)),
         ],
         compiler_params=pltpu.CompilerParams(vmem_limit_bytes=60 << 20),
     )(fields_out, eps_grad)

time: 47.4 us -> 46.7 us (0.985)
  the two profiles are of different devices: /device:TPU:9 before, /device:TPU:23 now
where the time goes in v6:
time: 46.7 us; the launch traced here: 46.5 us
  Pallas kernels  45.2 us (97%)
  between operations  1.29 us (3%)
    pallas_call x1, Pallas kernels, on_device(): pl.pallas_call(kernel, out_shape=(jax.ShapeDtypeStruct(fields_in.shape, f...  43.2 us
    pallas_call x1, Pallas kernels, on_device(): pl.pallas_call(hand_on, out_shape=(jax.ShapeDtypeStruct(fields_in.shape,...  2.05 us

profile of v6, /device:TPU:23, one launch (start us, length us, event | category | flops | bytes accessed | tf_op | source)
XLA Modules:
  0.0 46.5 jit_solution(1369195877522819610)
XLA Ops:
  1.3 43.2 %shard_map.86 = (f32[6,4,64,128]{3,2,1,0:T(8,128)}, f32[4,64,128]{2,1,0:T(8,128)}) custom-call(f32[4]{0:T(128)} %eps_ref.1, s32[1]{0:T(128)S(6)} %copy.9.plane_ref, f32[4]{0:T(128)} %wave_ref.1, f32[6,4,64,128]{3,2,1,0:T(8,128)} %fields.1, s32[4,64,128]{2,1,0:T(8,128)} %material.1, f32[64,128]{1,0:T(8,128)} %profile.1, bf16[4,3,4,64,128]{4,3,2,1,0:T(8,128)(2,1)} %forward.1), custom_call_target="tpu_custom_call" | custom-call | tf_op jit(solution)/shard_map/pallas_call | solution.py:549
  44.4 2.1 %shard_map.87 = (f32[6,4,64,128]{3,2,1,0:T(8,128)}, f32[4,64,128]{2,1,0:T(8,128)}) custom-call(f32[6,4,64,128]{3,2,1,0:T(8,128)} %get-tuple-element.4.fields, f32[4,64,128]{2,1,0:T(8,128)} %get-tuple-element.5.grad), custom_call_target="tpu_custom_call" | custom-call | tf_op jit(solution)/shard_map/pallas_call | solution.py:600

commit v7 on v6

--- a/solution.py
+++ b/solution.py
@@ -365,7 +365,7 @@
         if not outer:
             push(5, minus(next_x(ey), next_y(ex)))
 
-    def electric(p, t):
+    def electric(p, t, along=(0, 1, 2)):
         coef = ca[p], cb[p]
 
         def push(c, curl):
@@ -373,9 +373,9 @@
             put(c, p, tuple(o + k * d for o, k, d in zip(old, coef, curl)), t)
 
         hx, hy = pair(3, p), pair(4, p)
-        if not (isinstance(p, int) and p == top and t == STEPS - 1):
+        if 2 in along and not (isinstance(p, int) and p == top and t == STEPS - 1):
             push(2, minus(last_x(hy), last_y(hx)))
-        if isinstance(p, int) and p == 0:
+        if 0 not in along or isinstance(p, int) and p == 0:
             return
         hz = pair(5, p)
         here = (gz * depth + p - LOW == plane_ref[0]).astype(jnp.float32)
@@ -442,7 +442,7 @@
     magnetic(b, 1)
     electric(b, 1)
     magnetic(b - 1, 2)
-    electric(b - 1, 2)
+    electric(b - 1, 2, (0, 1))
     told_up = tell(2, (0,))
 
     for copy in rising + ghosts[2:] + borders[:1]:
@@ -454,8 +454,9 @@
     magnetic(1, 1)
     electric(a, 1)
     magnetic(a, 2)
-    electric(a + 1, 2)
+    electric(a + 1, 2, (0, 1))
     told_down = tell(2, (1,))
+    each((a + 1, b - 1), lambda p: electric(p, 2, (2,)))
     each((a, b), lambda p: gather(p, 1))
     run(a + 1, b, lambda p: gather(p, 2))
 

time: 46.7 us -> 46.7 us (level)
  no operation moved by 1% of the time
where the time goes in v7:
time: 46.7 us; the launch traced here: 46.5 us
  Pallas kernels  45.2 us (97%)
  between operations  1.29 us (3%)
    pallas_call x1, Pallas kernels, on_device(): pl.pallas_call(kernel, out_shape=(jax.ShapeDtypeStruct(fields_in.shape, f...  43.1 us
    pallas_call x1, Pallas kernels, on_device(): pl.pallas_call(hand_on, out_shape=(jax.ShapeDtypeStruct(fields_in.shape,...  2.05 us

profile of v7, /device:TPU:23, one launch (start us, length us, event | category | flops | bytes accessed | tf_op | source)
XLA Modules:
  0.0 46.5 jit_solution(3921915418857786892)
XLA Ops:
  1.3 43.1 %shard_map.86 = (f32[6,4,64,128]{3,2,1,0:T(8,128)}, f32[4,64,128]{2,1,0:T(8,128)}) custom-call(f32[4]{0:T(128)} %eps_ref.1, s32[1]{0:T(128)S(6)} %copy.9.plane_ref, f32[4]{0:T(128)} %wave_ref.1, f32[6,4,64,128]{3,2,1,0:T(8,128)} %fields.1, s32[4,64,128]{2,1,0:T(8,128)} %material.1, f32[64,128]{1,0:T(8,128)} %profile.1, bf16[4,3,4,64,128]{4,3,2,1,0:T(8,128)(2,1)} %forward.1), custom_call_target="tpu_custom_call" | custom-call | tf_op jit(solution)/shard_map/pallas_call | solution.py:550
  44.4 2.1 %shard_map.87 = (f32[6,4,64,128]{3,2,1,0:T(8,128)}, f32[4,64,128]{2,1,0:T(8,128)}) custom-call(f32[6,4,64,128]{3,2,1,0:T(8,128)} %get-tuple-element.4.fields, f32[4,64,128]{2,1,0:T(8,128)} %get-tuple-element.5.grad), custom_call_target="tpu_custom_call" | custom-call | tf_op jit(solution)/shard_map/pallas_call | solution.py:601
